TPU v7x, 32 devices: a whole 2x2x4 slice. The times are simulated.
32 devices in a mesh: slab: 2 (over x), page: 16 (over z, y, core).
Axes of the slice: x: 2, y: 2, z: 4, core: 2. Of those that a mesh axis runs over, the one named last changes fastest.
Arguments:
- latents: bfloat16 [128, 1024], P(('slab', 'page')), parts along dimension 0, may hold values from -6 to 6
- patches: bfloat16 [65536, 1024], P(('slab', 'page')), parts along dimension 0, may hold values from -6 to 6
- lat_gain: float32 [1024], replicated, may hold values from 0.1 to 1.9
- patch_gain: float32 [1024], replicated, may hold values from 0.1 to 1.9
- mlp_gain: float32 [1024], replicated, may hold values from 0.1 to 1.9
- w_query: bfloat16 [1024, 1024], replicated, may hold values from -0.5 to 0.5
- w_key: bfloat16 [1024, 1024], replicated, may hold values from -0.1875 to 0.1875
- w_value: bfloat16 [1024, 1024], replicated, may hold values from -0.1875 to 0.1875
- w_out: bfloat16 [1024, 1024], replicated, may hold values from -0.5 to 0.5
- w_hidden: bfloat16 [1024, 4096], P(None, 'page'), may hold values from -0.1875 to 0.1875
- w_connect: bfloat16 [4096, 4096], P(None, 'page'), may hold values from -0.09375 to 0.09375
Outputs:
- resampled: bfloat16 [128, 1024], P(('slab', 'page')), parts along dimension 0
- connector: bfloat16 [128, 4096], P('slab', 'page'), parts along dimension 0
There are 2 independent parts, one for each index of `slab`. A program takes and returns all parts, laid end to end along the dimension named above; an argument that names none is the same for every part. Nothing has to cross between parts.
All inputs are finite; a program needn't handle non-finite values.
Results may differ from a plain program's by a relative error of at most 0.012.
Values may be sent and summed in bfloat16 or wider, within the bound.
No kernel may reach another device: no remote copies, remote signals or barrier semaphores. Data moves between devices by JAX's collectives and lax.ppermute only.
A program may use at most 128 MiB of HBM per device.

v0:
```python
import math

import jax
import jax.numpy as jnp
from jax import lax
from jax.sharding import PartitionSpec as P

HEADS = 16


def norm_rows(values_in, gain):
    center = values_in - jnp.mean(values_in, axis=-1, keepdims=True)
    spread = jnp.mean(center * center, axis=-1, keepdims=True)
    return center * lax.rsqrt(spread + 1e-05) * gain


def attend_block(query_rows, keys, values, head_count):
    row_count = query_rows.shape[0]
    width = query_rows.shape[1]
    head_dim = width // head_count
    group_width = 2 * head_dim
    groups = head_count // 2
    scale = 1.0 / math.sqrt(head_dim)

    def head_pair(group):
        column = group * group_width
        query_part = lax.dynamic_slice_in_dim(query_rows, column, group_width, 1).reshape(
            row_count, 2, head_dim
        )
        key_part = lax.dynamic_slice_in_dim(keys, column, group_width, 1).reshape(
            keys.shape[0], 2, head_dim
        )
        value_part = lax.dynamic_slice_in_dim(values, column, group_width, 1).reshape(
            values.shape[0], 2, head_dim
        )
        scores = (
            jnp.einsum("lhd,phd->hlp", query_part, key_part, preferred_element_type=jnp.float32)
            * scale
        )
        expo = jnp.exp(scores)
        denom = jnp.sum(expo, axis=-1)
        probs = expo.astype(jnp.bfloat16)
        numer = jnp.einsum("hlp,phd->lhd", probs, value_part, preferred_element_type=jnp.float32)
        return (numer.reshape(row_count, group_width), denom)

    numers, denoms = lax.map(head_pair, jnp.arange(groups))
    numer = jnp.transpose(numers, (1, 0, 2)).reshape(row_count, width)
    denom = jnp.transpose(denoms.reshape(head_count, row_count))
    return (numer, denom)


def body(
    latents,
    patches,
    lat_gain,
    patch_gain,
    mlp_gain,
    w_query,
    w_key,
    w_value,
    w_out,
    w_hidden,
    w_connect,
):
    lat_rows = latents.shape[0]
    width = latents.shape[1]
    lat_norm = norm_rows(latents.astype(jnp.float32), lat_gain).astype(jnp.bfloat16)
    query = jnp.dot(lat_norm, w_query, preferred_element_type=jnp.float32).astype(jnp.bfloat16)
    query_all = lax.all_gather(query, "page", axis=0, tiled=True)
    patch_norm = norm_rows(patches.astype(jnp.float32), patch_gain).astype(jnp.bfloat16)
    keys = jnp.dot(patch_norm, w_key, preferred_element_type=jnp.float32).astype(jnp.bfloat16)
    values = jnp.dot(patch_norm, w_value, preferred_element_type=jnp.float32).astype(jnp.bfloat16)
    numer, denom = attend_block(query_all, keys, values, HEADS)
    numer_mine, denom_mine = (
        lax.psum_scatter(numer, "page", scatter_dimension=0, tiled=True),
        lax.psum_scatter(denom, "page", scatter_dimension=0, tiled=True),
    )
    head_dim = width // HEADS
    attended = (
        (numer_mine.reshape(lat_rows, HEADS, head_dim) / denom_mine[:, :, None])
        .reshape(lat_rows, width)
        .astype(jnp.bfloat16)
    )
    mixed = latents.astype(jnp.float32) + jnp.dot(
        attended, w_out, preferred_element_type=jnp.float32
    )
    resampled = mixed.astype(jnp.bfloat16)
    mlp_in = norm_rows(mixed, mlp_gain).astype(jnp.bfloat16)
    hidden = jax.nn.gelu(
        jnp.dot(
            lax.all_gather(mlp_in, "page", axis=0, tiled=True),
            w_hidden,
            preferred_element_type=jnp.float32,
        ),
        approximate=True,
    ).astype(jnp.bfloat16)
    connector = jnp.dot(
        lax.all_gather(hidden, "page", axis=1, tiled=True),
        w_connect,
        preferred_element_type=jnp.float32,
    ).astype(jnp.bfloat16)
    return (resampled, connector)


def solution(mesh):
    placed = (
        P(("slab", "page"), None),
        P(("slab", "page"), None),
        P(),
        P(),
        P(),
        P(),
        P(),
        P(),
        P(),
        P(None, "page"),
        P(None, "page"),
    )
    return jax.shard_map(
        body,
        mesh=mesh,
        in_specs=placed,
        out_specs=(P(("slab", "page"), None), P("slab", "page")),
        check_vma=False,
    )
```

profile of v0, /device:TPU:0, one launch (start us, length us, event | category | flops | bytes accessed | tf_op | source)
XLA Modules:
  0.0 254.9 jit_solution(5159464395260327961)
XLA Ops:
  7.3 3.0 %convert_reduce_fusion = f32[2048]{0:T(1024)S(1)} fusion(bf16[2048,1024]{1,0:T(8,128)(2,1)} %param.14), kind=kLoop, calls=%fused_computation.11 | loop fusion | flops 4192256 | bytes 4202496 | tf_op jit(solution)/shard_map/reduce_sum | solution.py:12
  10.8 1.4 fusion.6
  12.3 6.2 %convolution_convert_fusion = bf16[2048,1024]{1,0:T(8,128)(2,1)} fusion(bf16[1024,1024]{1,0:T(8,128)(2,1)S(1)} %copy-done, bf16[2048,1024]{1,0:T(8,128)(2,1)S(1)} %copy-done.1, f32[1024]{0:T(1024)S(1)} %copy-done.8, f32[2048]{0:T(1024)S(1)} %add_rsqrt_fusion, f32[2048]{0:T(1024)S(1)} %broadcast_multiply_fusion), kind=kOutput, calls=%fused_computation.17 | convolution fusion | flops 4307550208 | bytes 10506240 | tf_op jit(solution)/shard_map/dot_general | solution.py:71
  18.5 6.2 %convolution_convert_fusion.1 = bf16[2048,1024]{1,0:T(8,128)(2,1)} fusion(bf16[1024,1024]{1,0:T(8,128)(2,1)S(1)} %copy-done.7, bf16[2048,1024]{1,0:T(8,128)(2,1)S(1)} %copy-done.1, f32[1024]{0:T(1024)S(1)} %copy-done.8, f32[2048]{0:T(1024)S(1)} %add_rsqrt_fusion, f32[2048]{0:T(1024)S(1)} %broadcast_multiply_fusion), kind=kOutput, calls=%fused_computation.18 | convolution fusion | flops 4307550208 | bytes 10506240 | tf_op jit(solution)/shard_map/dot_general | solution.py:72
  25.4 23.4 %all-gather = bf16[16,4,1024]{2,1,0:T(4,128)(2,1)S(1)} all-gather(bf16[1,4,1024]{2,1,0:T(4,128)(2,1)S(1)} %fusion.9), channel_id=1, replica_groups=mesh['slab'=2,'page'=16] {'page'}, dimensions={0}, use_global_device_ids=true | all-gather | bytes 139264 | tf_op jit(solution)/shard_map/all_gather | solution.py:69
  48.9 64.3 %while.12 = (s32[]{:T(128)}, f32[8,64,128]{1,2,0:T(8,128)}, f32[8,2,64]{2,1,0:T(2,128)S(1)}, s32[8]{0:T(128)S(1)}, bf16[2048,1024]{1,0:T(8,128)(2,1)}, /*index=5...) while((s32[]{:T(128)}, f32[8,64,128]{1,2,0:T(8,128)}, ...), condition=%wide.region_6.7_spmd, body=%wide.region_4.6_spmd.sunk | while | flops 67895168 | bytes 6507699 | solution.py:46
  50.2 1.3 constant_dynamic-slice_fusion.6
  52.7 2.1 fusion.53
  55.0 1.3 fusion.54
  58.2 1.3 constant_dynamic-slice_fusion.6
  60.7 2.1 fusion.53
  63.1 1.3 fusion.54
  66.3 1.3 constant_dynamic-slice_fusion.6
  68.8 2.1 fusion.53
  71.1 1.3 fusion.54
  76.8 2.1 fusion.53
  79.1 1.3 fusion.54
  82.4 1.3 constant_dynamic-slice_fusion.6
  84.8 2.1 fusion.53
  87.2 1.3 fusion.54
  92.9 2.1 fusion.53
  95.2 1.3 fusion.54
  100.9 2.1 fusion.53
  103.2 1.3 fusion.54
  108.9 2.1 fusion.53
  111.3 1.3 fusion.54
  114.5 30.5 %all-reduce.1 = f32[64,16]{0,1:T(8,128)S(1)} all-reduce(f32[64,16]{0,1:T(8,128)S(1)} %bitcast.57), channel_id=3, replica_groups=mesh['slab'=2,'page'=16] {'page'}, use_global_device_ids=true, to_apply=%region_8.9.clone | all-reduce | flops 1024 | bytes 8192
  145.1 55.7 %all-reduce.4.cloned.1.call-done = f32[64,1024]{0,1:T(8,128)} async-done(((f32[64,1024]{0,1:T(8,128)}), f32[64,1024]{0,1:T(8,128)}) %all-reduce.4.cloned.1.call-update) | async-done | bytes 262160
  202.1 2.1 fusion.32
  205.0 21.2 %all-gather.1 = bf16[16,4,1024]{2,1,0:T(4,128)(2,1)S(1)} all-gather(bf16[1,4,1024]{2,1,0:T(4,128)(2,1)S(1)} %get-tuple-element.81), channel_id=1, replica_groups=mesh['slab'=2,'page'=16] {'page'}, dimensions={0}, use_global_device_ids=true | all-gather | bytes 139264 | tf_op jit(solution)/shard_map/all_gather | solution.py:91
  226.5 18.9 %all_gather.11 = bf16[64,4096]{1,0:T(8,128)(2,1)S(1)} all-gather(bf16[64,256]{1,0:T(8,128)(2,1)S(1)} %fusion.18), channel_id=1, replica_groups=mesh['slab'=2,'page'=16] {'page'}, dimensions={1}, use_global_device_ids=true | all-gather | bytes 557056 | tf_op jit(solution)/shard_map/all_gather | solution.py:98
  245.3 2.7 %convolution_convert_fusion.2 = bf16[64,256]{1,0:T(8,128)(2,1)} fusion(bf16[64,4096]{1,0:T(8,128)(2,1)S(1)} %all_gather.11, bf16[4096,256]{1,0:T(8,128)(2,1)} %param.23), kind=kOutput, calls=%fused_computation.19 | convolution fusion | flops 134234112 | bytes 2654208 | tf_op jit(solution)/shard_map/dot_general | solution.py:97
  (102 shorter events, 30.5 us)
Async XLA Ops:
  7.2 5.1 %copy-start = (bf16[1024,1024]{1,0:T(8,128)(2,1)S(1)}, bf16[1024,1024]{1,0:T(8,128)(2,1)}, u32[]{:S(2)}) copy-start(bf16[1024,1024]{1,0:T(8,128)(2,1)} %param.19) | copy-start | bytes 6291460
  7.2 193.6 %all-reduce.4.cloned.1.call-start = ((), (), s32[]{:S(2)}) async-start(), calls=%async_computation | async-start | bytes 1048576
  7.2 3.6 %copy-start.1 = (bf16[2048,1024]{1,0:T(8,128)(2,1)S(1)}, bf16[2048,1024]{1,0:T(8,128)(2,1)}, u32[]{:S(2)}) copy-start(bf16[2048,1024]{1,0:T(8,128)(2,1)} %param.14) | copy-start | bytes 12582916
  7.3 5.0 %copy-start.8 = (f32[1024]{0:T(1024)S(1)}, f32[1024]{0:T(1024)}, u32[]{:S(2)}) copy-start(f32[1024]{0:T(1024)} %param.16) | copy-start | bytes 12292
  12.3 6.2 %copy-start.7 = (bf16[1024,1024]{1,0:T(8,128)(2,1)S(1)}, bf16[1024,1024]{1,0:T(8,128)(2,1)}, u32[]{:S(2)}) copy-start(bf16[1024,1024]{1,0:T(8,128)(2,1)} %param.20) | copy-start | bytes 6291460
  18.5 6.2 %copy-start.4 = (bf16[4,1024]{1,0:T(4,128)(2,1)S(1)}, bf16[4,1024]{1,0:T(4,128)(2,1)}, u32[]{:S(2)}) copy-start(bf16[4,1024]{1,0:T(4,128)(2,1)} %param.13) | copy-start | bytes 24580
  18.5 6.5 %copy-start.2 = (bf16[1024,1024]{1,0:T(8,128)(2,1)S(1)}, bf16[1024,1024]{1,0:T(8,128)(2,1)}, u32[]{:S(2)}) copy-start(bf16[1024,1024]{1,0:T(8,128)(2,1)} %param.18) | copy-start | bytes 6291460
  18.5 6.5 %copy-start.5 = (f32[1024]{0:T(1024)S(1)}, f32[1024]{0:T(1024)}, u32[]{:S(2)}) copy-start(f32[1024]{0:T(1024)} %param.15) | copy-start | bytes 12292
  48.9 64.4 %copy-start.9 = (u32[32]{0:T(128)S(1)}, u32[32]{0:T(128)}, u32[]{:S(2)}) copy-start(u32[32]{0:T(128)} %constant.48) | copy-start | bytes 388
  48.9 155.5 %copy-start.6 = (f32[1024]{0:T(1024)S(1)}, f32[1024]{0:T(1024)}, u32[]{:S(2)}) copy-start(f32[1024]{0:T(1024)} %param.17) | copy-start | bytes 12292
  113.2 113.0 %copy-start.3 = (bf16[1024,256]{1,0:T(8,128)(2,1)S(1)}, bf16[1024,256]{1,0:T(8,128)(2,1)}, u32[]{:S(2)}) copy-start(bf16[1024,256]{1,0:T(8,128)(2,1)} %param.22) | copy-start | bytes 1572868
Sparse Core Ops, SparseCore 0:
  113.4 87.3 all-reduce.3
where the time goes:
time: 256 us; the launch traced here: 255 us
  blocking collectives  94 us (37%)
  waiting for transfers between devices  55.7 us (22%)
  matrix products  45.5 us (18%)
  local copies, waits for them, and re-layouts  32.6 us (13%)
  between operations  14.9 us (6%)
  other arithmetic  6.74 us (3%)
  loops' own time  5.42 us (2%)
    unnamed x2, waiting for transfers between devices  55.7 us
    unnamed x1, blocking collectives  30.5 us
    all_gather x1, blocking collectives, body(): query_all = lax.all_gather(query, 'page', axis=0, tiled=True)  23.4 us
    all_gather x1, blocking collectives, body(): lax.all_gather(mlp_in, 'page', axis=0, tiled=True)  21.2 us
    dynamic_slice x16, local copies, waits for them, and re-layouts, head_pair(): lax.dynamic_slice_in_dim(keys, column, group_width, 1)  19 us
    all_gather x1, blocking collectives, body(): lax.all_gather(hidden, 'page', axis=1, tiled=True)  18.9 us
    dot_general x8, matrix products, head_pair(): jnp.einsum('lhd,phd->hlp', query_part, key_part, preferred_element_type=j...  17.1 us
    dot_general x8, matrix products, head_pair(): jnp.einsum('hlp,phd->lhd', probs, value_part, preferred_element_type=jnp....  10.6 us
  transfers between devices with their start and end apart: 1, of which 1 were waited for; matrix products, arithmetic and copies ran while one was open for 0% of the time, Pallas kernels for 0%

commit v1 on v0

v1 whole, which is shorter than its diff:
```python
import math

import jax
import jax.numpy as jnp
from jax import lax
from jax.experimental import pallas as pl
from jax.experimental.pallas import tpu as pltpu
from jax.sharding import PartitionSpec as P

HEADS = 16
PACK = 4
LANES = 128


def norm_rows(values_in, gain):
    center = values_in - jnp.mean(values_in, axis=-1, keepdims=True)
    spread = jnp.mean(center * center, axis=-1, keepdims=True)
    return center * lax.rsqrt(spread + 1e-05) * gain


def attend_kernel(x_ref, gain_ref, wk_ref, wv_ref, q_ref, num_ref, den_ref, qbd, acc, dacc):
    step = pl.program_id(0)
    block = x_ref.shape[0]
    latents, width = q_ref.shape
    head_dim = width // HEADS
    span = PACK * head_dim
    groups = HEADS // PACK
    lane_head = lax.broadcasted_iota(jnp.int32, (latents, span), 1) // head_dim

    @pl.when(step == 0)
    def _():
        acc[...] = jnp.zeros_like(acc)
        dacc[...] = jnp.zeros_like(dacc)
        for g in range(groups):
            part = q_ref[:, g * span : (g + 1) * span]
            for h in range(PACK):
                qbd[g, h * latents : (h + 1) * latents, :] = jnp.where(
                    lane_head == h, part, jnp.zeros_like(part)
                )

    x = x_ref[...].astype(jnp.float32)
    pn = norm_rows(x, gain_ref[...]).astype(jnp.bfloat16)
    keys = jnp.dot(pn, wk_ref[...], preferred_element_type=jnp.float32).astype(jnp.bfloat16)
    values = jnp.dot(pn, wv_ref[...], preferred_element_type=jnp.float32).astype(jnp.bfloat16)
    factor = math.log2(math.e) / math.sqrt(head_dim)
    for g in range(groups):
        cols = slice(g * span, (g + 1) * span)
        scores = lax.dot_general(
            qbd[g], keys[:, cols], (((1,), (1,)), ((), ())), preferred_element_type=jnp.float32
        )
        expo = jnp.exp2(scores * factor)
        total = expo[:, :LANES]
        for j in range(1, block // LANES):
            total = total + expo[:, j * LANES : (j + 1) * LANES]
        dacc[g] += total
        acc[g] += jnp.dot(
            expo.astype(jnp.bfloat16), values[:, cols], preferred_element_type=jnp.float32
        )

    @pl.when(step == pl.num_programs(0) - 1)
    def _():
        lane = lax.broadcasted_iota(jnp.int32, (latents, LANES), 1)
        out = jnp.zeros((latents, LANES), jnp.float32)
        for g in range(groups):
            sums = jnp.sum(dacc[g], axis=-1, keepdims=True)
            picked = jnp.zeros((latents, span), jnp.float32)
            for h in range(PACK):
                rows = slice(h * latents, (h + 1) * latents)
                picked = jnp.where(lane_head == h, acc[g, rows, :], picked)
                out = jnp.where(lane == g * PACK + h, sums[rows], out)
            num_ref[:, g * span : (g + 1) * span] = picked
        den_ref[...] = out


def attend(patches, gain, w_key, w_value, query):
    rows, width = patches.shape
    latents = query.shape[0]
    block = 256
    span = PACK * (width // HEADS)
    groups = HEADS // PACK
    whole = lambda shape: pl.BlockSpec(shape, lambda i: (0,) * len(shape))
    once = lambda shape: pl.BlockSpec(
        shape, lambda i: (0,) * len(shape), pipeline_mode=pl.Buffered(1)
    )
    return pl.pallas_call(
        attend_kernel,
        grid=(rows // block,),
        in_specs=[
            pl.BlockSpec((block, width), lambda i: (i, 0)),
            once((1, width)),
            once((width, width)),
            once((width, width)),
            once((latents, width)),
        ],
        out_specs=[whole((latents, width)), whole((latents, LANES))],
        out_shape=[
            jax.ShapeDtypeStruct((latents, width), jnp.float32),
            jax.ShapeDtypeStruct((latents, LANES), jnp.float32),
        ],
        scratch_shapes=[
            pltpu.VMEM((groups, PACK * latents, span), jnp.bfloat16),
            pltpu.VMEM((groups, PACK * latents, span), jnp.float32),
            pltpu.VMEM((groups, PACK * latents, LANES), jnp.float32),
        ],
        compiler_params=pltpu.CompilerParams(
            dimension_semantics=("arbitrary",), vmem_limit_bytes=48 * 1024 * 1024
        ),
        cost_estimate=pl.CostEstimate(
            flops=4 * rows * width * width + 4 * rows * latents * PACK * width,
            transcendentals=rows * latents * HEADS,
            bytes_accessed=2 * rows * width + 4 * width * width,
        ),
        name="attend",
    )(patches, gain.reshape(1, width), w_key, w_value, query)


def spread_rows(block, count):
    everyone = jnp.broadcast_to(block[None], (count,) + block.shape)
    return lax.all_to_all(everyone, "page", 0, 0, tiled=True)


def body(
    latents,
    patches,
    lat_gain,
    patch_gain,
    mlp_gain,
    w_query,
    w_key,
    w_value,
    w_out,
    w_hidden,
    w_connect,
):
    count = lax.axis_size("page")
    lat_rows, width = latents.shape
    head_dim = width // HEADS
    lat_norm = norm_rows(latents.astype(jnp.float32), lat_gain).astype(jnp.bfloat16)
    query = jnp.dot(lat_norm, w_query, preferred_element_type=jnp.float32).astype(jnp.bfloat16)
    query_all = spread_rows(query, count).reshape(count * lat_rows, width)
    numer, denom = attend(patches, patch_gain, w_key, w_value, query_all)
    packed = jnp.concatenate([numer, denom], axis=1).reshape(count, lat_rows, width + LANES)
    summed = jnp.sum(lax.all_to_all(packed, "page", 0, 0, tiled=True), axis=0)
    attended = (
        (summed[:, :width].reshape(lat_rows, HEADS, head_dim) / summed[:, width : width + HEADS, None])
        .reshape(lat_rows, width)
        .astype(jnp.bfloat16)
    )
    mixed = latents.astype(jnp.float32) + jnp.dot(
        attended, w_out, preferred_element_type=jnp.float32
    )
    resampled = mixed.astype(jnp.bfloat16)
    mlp_in = norm_rows(mixed, mlp_gain).astype(jnp.bfloat16)
    mlp_all = spread_rows(mlp_in, count).reshape(count * lat_rows, width)
    hidden = jax.nn.gelu(
        jnp.dot(mlp_all, w_hidden, preferred_element_type=jnp.float32), approximate=True
    ).astype(jnp.bfloat16)
    units = hidden.shape[1]
    hidden_all = spread_rows(hidden, count)
    connector = lax.dot_general(
        jnp.transpose(hidden_all, (1, 0, 2)).reshape(hidden.shape[0], count * units),
        w_connect,
        (((1,), (0,)), ((), ())),
        preferred_element_type=jnp.float32,
    ).astype(jnp.bfloat16)
    return (resampled, connector)


def solution(mesh):
    placed = (
        P(("slab", "page"), None),
        P(("slab", "page"), None),
        P(),
        P(),
        P(),
        P(),
        P(),
        P(),
        P(),
        P(None, "page"),
        P(None, "page"),
    )
    return jax.shard_map(
        body,
        mesh=mesh,
        in_specs=placed,
        out_specs=(P(("slab", "page"), None), P("slab", "page")),
        check_vma=False,
    )
```

time: 256 us -> 86.5 us (0.34)
  waiting for transfers between devices: 55.7 us -> 0 us
  matrix products: 45.5 us -> 5.44 us
  blocking collectives: 94 us -> 56.3 us
  local copies, waits for them, and re-layouts: 32.6 us -> 3.68 us
  Pallas kernels: 0 us -> 17.1 us
  between operations: 14.9 us -> 0.78 us
  loops' own time: 5.42 us -> 0 us
  other arithmetic: 6.74 us -> 2.77 us
    all_gather x3 -> x0, blocking collectives: 63.5 us -> none  [the longest x1 23.4 us: body(): query_all = lax.all_gather(query, 'page', axis=0, tiled=True)]
    all_to_all x0 -> x4, blocking collectives: none -> 56.3 us  [the longest x3 43 us: spread_rows(): return lax.all_to_all(everyone, 'page', 0, 0, tiled=True)]
    unnamed x2 -> x0, waiting for transfers between devices: 55.7 us -> none
    dot_general x20 -> x2, matrix products: 43 us -> 1.3 us  [the longest x1 1.08 us: body(): lax.dot_general(jnp.transpose(hidden_all, (1, 0, 2)).reshape(hidden.shape...]
    unnamed x1 -> x0, blocking collectives: 30.5 us -> none
    dynamic_slice x40 -> x0, local copies, waits for them, and re-layouts: 25.4 us -> none  [the longest x16 19 us: head_pair(): lax.dynamic_slice_in_dim(keys, column, group_width, 1)]
    pallas_call x0 -> x1, Pallas kernels: none -> 17.1 us  [attend(): pl.pallas_call(attend_kernel, grid=(rows // block,), in_specs=[pl.BlockSp...]
    another operation x1 -> x0, loops' own time: 5.42 us -> none  [attend_block(): numers, denoms = lax.map(head_pair, jnp.arange(groups))]
  transfers between devices with their start and end apart: 1 -> 0, of which waited for: 1 -> 0; matrix products, arithmetic and copies ran while one was open for 0% -> 0% of each run, Pallas kernels for 0% -> 0%
where the time goes in v1:
time: 86.5 us; the launch traced here: 86.1 us
  blocking collectives  56.3 us (65%)
  Pallas kernels  17.1 us (20%)
  matrix products  5.44 us (6%)
  local copies, waits for them, and re-layouts  3.68 us (4%)
  other arithmetic  2.77 us (3%)
    all_to_all x3, blocking collectives, spread_rows(): return lax.all_to_all(everyone, 'page', 0, 0, tiled=True)  43 us
    pallas_call x1, Pallas kernels, attend(): pl.pallas_call(attend_kernel, grid=(rows // block,), in_specs=[pl.BlockSp...  17.1 us
    all_to_all x1, blocking collectives, body(): summed = jnp.sum(lax.all_to_all(packed, 'page', 0, 0, tiled=True), axis=0)  13.3 us
    unnamed x14, local copies, waits for them, and re-layouts  3.21 us
    dot_general x1, matrix products, body(): jnp.dot(attended, w_out, preferred_element_type=jnp.float32)  2.09 us
    dot_general x1, matrix products, body(): jnp.dot(lat_norm, w_query, preferred_element_type=jnp.float32)  2.05 us

profile of v1, /device:TPU:0, one launch (start us, length us, event | category | flops | bytes accessed | tf_op | source)
XLA Modules:
  0.0 86.1 jit_solution(11020944907712233155)
XLA Ops:
  0.6 0.0 copy-start
  0.6 0.0 copy-start.3
  0.7 1.0 %convert_reduce_fusion = f32[4]{0:T(128)S(1)} fusion(bf16[4,1024]{1,0:T(4,128)(2,1)} %param.11), kind=kLoop, calls=%fused_computation.14 | loop fusion | flops 8188 | bytes 8208 | tf_op jit(solution)/shard_map/reduce_sum | solution.py:16
  1.6 0.9 %fusion.10 = f32[4]{0:T(128)S(1)} fusion(bf16[4,1024]{1,0:T(4,128)(2,1)} %param.11, f32[4]{0:T(128)S(1)} %broadcast_multiply_fusion.1), kind=kLoop, calls=%fused_computation.17 | loop fusion | flops 16380 | bytes 8224 | tf_op jit(solution)/shard_map/reduce_sum | solution.py:17
  2.5 2.0 %convolution_convert_fusion.1 = bf16[4,1024]{1,0:T(4,128)(2,1)S(1)} fusion(bf16[1024,1024]{1,0:T(8,128)(2,1)} %param.16, bf16[4,1024]{1,0:T(4,128)(2,1)} %param.11, f32[1024]{0:T(1024)} %param.13, f32[4]{0:T(128)S(1)} %add_rsqrt_fusion.1, f32[4]{0:T(128)S(1)} %broadcast_multiply_fusion.1), kind=kOutput, calls=%fused_computation.2 | convolution fusion | flops 8413184 | bytes 2117664 | tf_op jit(solution)/shard_map/dot_general | solution.py:139
  4.6 15.1 %all_to_all.20 = bf16[16,4,1024]{2,1,0:T(4,128)(2,1)S(1)} all-to-all(bf16[16,4,1024]{2,1,0:T(4,128)(2,1)S(1)} %broadcast_in_dim.6), channel_id=1, replica_groups=mesh['slab'=2,'page'=16] {'page'}, dimensions={0} | all-to-all | bytes 262144 | tf_op jit(solution)/shard_map/all_to_all | solution.py:119
  19.8 0.0 copy-done.3
  19.8 0.0 copy-start.1
  19.8 1.6 %copy-done.1 = bf16[1024,1024]{1,0:T(8,128)(2,1)S(1)} copy-done((bf16[1024,1024]{1,0:T(8,128)(2,1)S(1)}, bf16[1024,1024]{1,0:T(8,128)(2,1)}, u32[]{:S(2)}) %copy-start.1) | copy-done | bytes 2097176
  21.4 0.0 copy-start.2
  21.4 1.6 %copy-done.2 = bf16[1024,1024]{1,0:T(8,128)(2,1)S(1)} copy-done((bf16[1024,1024]{1,0:T(8,128)(2,1)S(1)}, bf16[1024,1024]{1,0:T(8,128)(2,1)}, u32[]{:S(2)}) %copy-start.2) | copy-done | bytes 2097176
  23.0 17.1 %attend.1 = (f32[64,1024]{1,0:T(8,128)S(1)}, f32[64,128]{1,0:T(8,128)S(1)}) custom-call(bf16[2048,1024]{1,0:T(8,128)(2,1)} %x_ref.1, f32[1,1024]{1,0:T(1,128)S(1)} %bitcast.10, bf16[1024,1024]{1,0:T(8,128)(2,1)S(1)} %copy-done.1, bf16[1024,1024]{1,0:T(8,128)(2,1)S(1)} %copy-done.2, bf16[64,1024]{1,0:T(8,128)(2,1)S(1)} %reshape.53.q_ref), custom_call_target="tpu_custom_call" | custom-call | flops 10737418240 | bytes 8388608 | tf_op jit(solution)/shard_map/attend/pallas_call | solution.py:85
  40.0 0.0 copy-start.5
  40.1 0.0 copy-start.6
  40.1 0.0 copy-start.4
  40.1 0.1 reshape.54
  40.2 13.3 %all_to_all.21 = f32[16,4,1152]{2,1,0:T(4,128)S(1)} all-to-all(f32[16,4,1152]{2,1,0:T(4,128)S(1)} %reshape.54), channel_id=1, replica_groups=mesh['slab'=2,'page'=16] {'page'}, dimensions={0} | all-to-all | bytes 589824 | tf_op jit(solution)/shard_map/all_to_all | solution.py:143
  53.5 0.1 reduce_sum.47
  53.6 0.1 div.25
  53.6 0.1 div.26
  53.7 0.0 copy-done.5
  53.7 2.1 %fusion.19 = (f32[4]{0:T(128)S(1)}, f32[4,1024]{1,0:T(4,128)S(1)}) fusion(bf16[1024,1024]{1,0:T(8,128)(2,1)} %param.19, f32[4,1024]{1,0:T(4,128)S(1)} %div.26, f32[4,1152]{1,0:T(4,128)S(1)} %reduce_sum.47, bf16[4,1024]{1,0:T(4,128)(2,1)S(1)} %copy-done.5), kind=kOutput, calls=%fused_computation.31 | convolution fusion | flops 8409084 | bytes 2154512 | tf_op jit(solution)/shard_map/dot_general | solution.py:149
  55.8 0.2 multiply_reduce_fusion
  56.0 0.0 copy-done.6
  56.0 0.6 multiply_convert_fusion
  56.7 10.8 %all_to_all.22 = bf16[16,4,1024]{2,1,0:T(4,128)(2,1)S(1)} all-to-all(bf16[16,4,1024]{2,1,0:T(4,128)(2,1)S(1)} %broadcast_in_dim.7), channel_id=1, replica_groups=mesh['slab'=2,'page'=16] {'page'}, dimensions={0} | all-to-all | bytes 262144 | tf_op jit(solution)/shard_map/all_to_all | solution.py:119
  67.6 0.0 copy-done.4
  67.6 0.2 fusion.7
  67.9 17.1 %all_to_all.23 = bf16[16,64,256]{2,1,0:T(8,128)(2,1)S(1)} all-to-all(bf16[16,64,256]{2,1,0:T(8,128)(2,1)S(1)} %broadcast_in_dim.8), channel_id=1, replica_groups=mesh['slab'=2,'page'=16] {'page'}, dimensions={0} | all-to-all | bytes 1048576 | tf_op jit(solution)/shard_map/all_to_all | solution.py:119
  85.0 0.0 copy-done
  85.0 1.1 %convolution_convert_fusion = bf16[64,256]{1,0:T(8,128)(2,1)} fusion(bf16[64,4096]{1,0:T(8,128)(2,1)S(1)} %bitcast.12, bf16[4096,256]{1,0:T(8,128)(2,1)S(1)} %copy-done), kind=kOutput, calls=%fused_computation | convolution fusion | flops 134234112 | bytes 2654208 | tf_op jit(solution)/shard_map/dot_general | solution.py:160
  (12 shorter events, 0.3 us)
Async XLA Ops:
  0.6 84.4 %copy-start = (bf16[4096,256]{1,0:T(8,128)(2,1)S(1)}, bf16[4096,256]{1,0:T(8,128)(2,1)}, u32[]{:S(2)}) copy-start(bf16[4096,256]{1,0:T(8,128)(2,1)} %param.21) | copy-start | bytes 6291460
  0.6 19.1 %copy-start.3 = (f32[1024]{0:T(1024)S(1)}, f32[1024]{0:T(1024)}, u32[]{:S(2)}) copy-start(f32[1024]{0:T(1024)} %param.14) | copy-start | bytes 12292
  19.8 1.6 %copy-start.1 = (bf16[1024,1024]{1,0:T(8,128)(2,1)S(1)}, bf16[1024,1024]{1,0:T(8,128)(2,1)}, u32[]{:S(2)}) copy-start(bf16[1024,1024]{1,0:T(8,128)(2,1)} %wk_ref.1) | copy-start | bytes 6291460
  21.4 1.6 %copy-start.2 = (bf16[1024,1024]{1,0:T(8,128)(2,1)S(1)}, bf16[1024,1024]{1,0:T(8,128)(2,1)}, u32[]{:S(2)}) copy-start(bf16[1024,1024]{1,0:T(8,128)(2,1)} %wv_ref.1) | copy-start | bytes 6291460
  40.0 13.7 %copy-start.5 = (bf16[4,1024]{1,0:T(4,128)(2,1)S(1)}, bf16[4,1024]{1,0:T(4,128)(2,1)}, u32[]{:S(2)}) copy-start(bf16[4,1024]{1,0:T(4,128)(2,1)} %param.11) | copy-start | bytes 24580
  40.1 16.0 %copy-start.6 = (f32[1024]{0:T(1024)S(1)}, f32[1024]{0:T(1024)}, u32[]{:S(2)}) copy-start(f32[1024]{0:T(1024)} %param.15) | copy-start | bytes 12292
  40.1 27.5 %copy-start.4 = (bf16[1024,256]{1,0:T(8,128)(2,1)S(1)}, bf16[1024,256]{1,0:T(8,128)(2,1)}, u32[]{:S(2)}) copy-start(bf16[1024,256]{1,0:T(8,128)(2,1)} %param.20) | copy-start | bytes 1572868

commit v2 on v1

v2 whole, which is shorter than its diff:
```python
import math

import jax
import jax.numpy as jnp
from jax import lax
from jax.experimental import pallas as pl
from jax.experimental.pallas import tpu as pltpu
from jax.sharding import PartitionSpec as P

HEADS = 16
PACK = 4
LANES = 128
MIB = 1024 * 1024


def norm_rows(values_in, gain):
    center = values_in - jnp.mean(values_in, axis=-1, keepdims=True)
    spread = jnp.mean(center * center, axis=-1, keepdims=True)
    return center * lax.rsqrt(spread + 1e-05) * gain


def in_hbm(array):
    return pltpu.with_memory_space_constraint(array, pltpu.HBM)


def fixed(shape):
    return pl.BlockSpec(shape, lambda i: (0,) * len(shape), pipeline_mode=pl.Buffered(1))


def project_kernel(x_ref, gain_ref, wk_ref, wv_ref, k_ref, v_ref):
    x = x_ref[...].astype(jnp.float32)
    pn = norm_rows(x, gain_ref[...]).astype(jnp.bfloat16)
    k_ref[...] = jnp.dot(pn, wk_ref[...], preferred_element_type=jnp.float32).astype(jnp.bfloat16)
    v_ref[...] = jnp.dot(pn, wv_ref[...], preferred_element_type=jnp.float32).astype(jnp.bfloat16)


def project(patches, gain, w_key, w_value):
    rows, width = patches.shape
    block = math.gcd(rows, 512)
    tile = pl.BlockSpec((block, width), lambda i: (i, 0))
    return pl.pallas_call(
        project_kernel,
        grid=(rows // block,),
        in_specs=[tile, fixed((1, width)), fixed((width, width)), fixed((width, width))],
        out_specs=[tile, tile],
        out_shape=[pltpu.HBM((rows, width), jnp.bfloat16)] * 2,
        compiler_params=pltpu.CompilerParams(
            dimension_semantics=("arbitrary",), vmem_limit_bytes=26 * MIB
        ),
        cost_estimate=pl.CostEstimate(
            flops=4 * rows * width * width,
            transcendentals=rows,
            bytes_accessed=6 * rows * width + 4 * width * width,
        ),
        name="project",
    )(in_hbm(patches), gain.reshape(1, width), in_hbm(w_key), in_hbm(w_value))


def attend_kernel(lat_ref, gain_ref, wq_ref, k_ref, v_ref, out_ref, qbd, acc, dacc):
    step = pl.program_id(0)
    block = k_ref.shape[0]
    latents, width = lat_ref.shape
    head_dim = width // HEADS
    span = PACK * head_dim
    groups = HEADS // PACK
    lane_head = lax.broadcasted_iota(jnp.int32, (latents, span), 1) // head_dim

    @pl.when(step == 0)
    def _():
        acc[...] = jnp.zeros_like(acc)
        dacc[...] = jnp.zeros_like(dacc)
        lat_norm = norm_rows(lat_ref[...].astype(jnp.float32), gain_ref[...]).astype(jnp.bfloat16)
        query = jnp.dot(lat_norm, wq_ref[...], preferred_element_type=jnp.float32)
        for g in range(groups):
            part = query[:, g * span : (g + 1) * span]
            for h in range(PACK):
                qbd[g, h * latents : (h + 1) * latents, :] = jnp.where(
                    lane_head == h, part, jnp.zeros_like(part)
                ).astype(jnp.bfloat16)

    factor = math.log2(math.e) / math.sqrt(head_dim)
    for g in range(groups):
        cols = slice(g * span, (g + 1) * span)
        scores = lax.dot_general(
            qbd[g], k_ref[:, cols], (((1,), (1,)), ((), ())), preferred_element_type=jnp.float32
        )
        expo = jnp.exp2(scores * factor)
        total = expo[:, :LANES]
        for j in range(1, block // LANES):
            total = total + expo[:, j * LANES : (j + 1) * LANES]
        dacc[g] += total
        acc[g] += jnp.dot(
            expo.astype(jnp.bfloat16), v_ref[:, cols], preferred_element_type=jnp.float32
        )

    @pl.when(step == pl.num_programs(0) - 1)
    def _():
        lane = lax.broadcasted_iota(jnp.int32, (latents, LANES), 1)
        out = jnp.zeros((latents, LANES), jnp.float32)
        for g in range(groups):
            sums = jnp.sum(dacc[g], axis=-1, keepdims=True)
            high = sums.astype(jnp.bfloat16).astype(jnp.float32)
            low = sums - high
            picked = jnp.zeros((latents, span), jnp.float32)
            for h in range(PACK):
                rows = slice(h * latents, (h + 1) * latents)
                picked = jnp.where(lane_head == h, acc[g, rows, :], picked)
                out = jnp.where(lane == g * PACK + h, high[rows], out)
                out = jnp.where(lane == HEADS + g * PACK + h, low[rows], out)
            out_ref[:, g * span : (g + 1) * span] = picked.astype(jnp.bfloat16)
        out_ref[:, width:] = out.astype(jnp.bfloat16)


def attend(latents, gain, w_query, keys, values):
    rows, width = keys.shape
    count = latents.shape[0]
    block = math.gcd(rows, 512)
    span = PACK * (width // HEADS)
    groups = HEADS // PACK
    tile = pl.BlockSpec((block, width), lambda i: (i, 0))
    return pl.pallas_call(
        attend_kernel,
        grid=(rows // block,),
        in_specs=[fixed((count, width)), fixed((1, width)), fixed((width, width)), tile, tile],
        out_specs=pl.BlockSpec((count, width + LANES), lambda i: (0, 0)),
        out_shape=jax.ShapeDtypeStruct((count, width + LANES), jnp.bfloat16),
        scratch_shapes=[
            pltpu.VMEM((groups, PACK * count, span), jnp.bfloat16),
            pltpu.VMEM((groups, PACK * count, span), jnp.float32),
            pltpu.VMEM((groups, PACK * count, LANES), jnp.float32),
        ],
        compiler_params=pltpu.CompilerParams(
            dimension_semantics=("arbitrary",), vmem_limit_bytes=44 * MIB
        ),
        cost_estimate=pl.CostEstimate(
            flops=4 * rows * count * PACK * width,
            transcendentals=rows * count * HEADS,
            bytes_accessed=4 * rows * width + 2 * width * width,
        ),
        name="attend",
    )(latents, gain.reshape(1, width), in_hbm(w_query), in_hbm(keys), in_hbm(values))


def mix_kernel(parts_ref, lat_ref, wo_ref, gain_ref, res_ref, mlp_ref):
    rows, width = lat_ref.shape
    head_dim = width // HEADS
    total = parts_ref[0].astype(jnp.float32)
    for j in range(1, parts_ref.shape[0]):
        total = total + parts_ref[j].astype(jnp.float32)
    denom = total[:, width : width + HEADS] + total[:, width + HEADS : width + 2 * HEADS]
    wide = jnp.concatenate(
        [jnp.broadcast_to(denom[:, h : h + 1], (rows, head_dim)) for h in range(HEADS)], axis=1
    )
    attended = (total[:, :width] / wide).astype(jnp.bfloat16)
    mixed = lat_ref[...].astype(jnp.float32) + jnp.dot(
        attended, wo_ref[...], preferred_element_type=jnp.float32
    )
    res_ref[...] = mixed.astype(jnp.bfloat16)
    mlp_ref[...] = norm_rows(mixed, gain_ref[...]).astype(jnp.bfloat16)


def mix(parts, latents, w_out, gain):
    rows, width = latents.shape
    return pl.pallas_call(
        mix_kernel,
        out_shape=[jax.ShapeDtypeStruct((rows, width), jnp.bfloat16)] * 2,
        cost_estimate=pl.CostEstimate(
            flops=2 * rows * width * width,
            transcendentals=rows,
            bytes_accessed=2 * width * width + 2 * parts.size,
        ),
        name="mix",
    )(parts, latents, w_out, gain.reshape(1, width))


def spread_rows(block, count):
    everyone = jnp.broadcast_to(block[None], (count,) + block.shape)
    return lax.all_to_all(everyone, "page", 0, 0, tiled=True)


def spread_pairs(block, count):
    chips = count // 2
    sides = [[2 * chip + side for chip in range(chips)] for side in range(2)]
    everyone = jnp.broadcast_to(block[None], (chips,) + block.shape)
    mine = lax.all_to_all(everyone, "page", 0, 0, axis_index_groups=sides, tiled=True)
    theirs = lax.ppermute(mine, "page", [(i, i ^ 1) for i in range(count)])
    return mine, theirs


def body(
    latents,
    patches,
    lat_gain,
    patch_gain,
    mlp_gain,
    w_query,
    w_key,
    w_value,
    w_out,
    w_hidden,
    w_connect,
):
    count = lax.axis_size("page")
    lat_rows, width = latents.shape
    lat_all = spread_rows(latents, count).reshape(count * lat_rows, width)
    keys, values = project(patches, patch_gain, w_key, w_value)
    packed = attend(lat_all, lat_gain, w_query, keys, values)
    parts = lax.all_to_all(
        packed.reshape(count, lat_rows, width + LANES), "page", 0, 0, tiled=True
    )
    resampled, mlp_in = mix(parts, latents, w_out, mlp_gain)
    mlp_all = spread_rows(mlp_in, count).reshape(count * lat_rows, width)
    hidden = jax.nn.gelu(
        jnp.dot(mlp_all, w_hidden, preferred_element_type=jnp.float32), approximate=True
    ).astype(jnp.bfloat16)
    rows, units = hidden.shape
    mine, theirs = spread_pairs(hidden, count)
    even = lax.axis_index("page") % 2 == 0
    both = jnp.stack([jnp.where(even, mine, theirs), jnp.where(even, theirs, mine)], axis=1)
    hidden_all = jnp.transpose(both.reshape(count, rows, units), (1, 0, 2)).reshape(
        rows, count * units
    )
    connector = jnp.dot(hidden_all, w_connect, preferred_element_type=jnp.float32).astype(
        jnp.bfloat16
    )
    return (resampled, connector)


def solution(mesh):
    placed = (
        P(("slab", "page"), None),
        P(("slab", "page"), None),
        P(),
        P(),
        P(),
        P(),
        P(),
        P(),
        P(),
        P(None, "page"),
        P(None, "page"),
    )
    return jax.shard_map(
        body,
        mesh=mesh,
        in_specs=placed,
        out_specs=(P(("slab", "page"), None), P("slab", "page")),
        check_vma=False,
    )
```

time: 86.5 us -> 76.1 us (0.88)
  blocking collectives: 56.3 us -> 36 us
  Pallas kernels: 17.1 us -> 25.4 us
  starting transfers between devices: 0 us -> 7.39 us
  matrix products: 5.44 us -> 1.3 us
  other arithmetic: 2.77 us -> 0.09 us
  waiting for transfers between devices: 0 us -> 1.54 us
    all_to_all x3 -> x1, blocking collectives: 43 us -> 10.5 us  [spread_rows(): return lax.all_to_all(everyone, 'page', 0, 0, tiled=True)]
    all_to_all x1 -> x2, blocking collectives: 13.3 us -> 25.5 us  [the longest x1 14.2 us: body(): lax.all_to_all(packed.reshape(count, lat_rows, width + LANES), 'page', 0,...]
    pallas_call x1 -> x3, Pallas kernels: 17.1 us -> 25.4 us  [the longest x1 14.9 us: project(): pl.pallas_call(project_kernel, grid=(rows // block,), in_specs=[tile, fix...]
    all_to_all x0 -> x1, starting transfers between devices: none -> 7.39 us  [spread_rows(): return lax.all_to_all(everyone, 'page', 0, 0, tiled=True)]
    dot_general x3 -> x1, matrix products: 5.22 us -> 1.08 us  [body(): jnp.dot(hidden_all, w_connect, preferred_element_type=jnp.float32)]
    unnamed x14 -> x8, local copies, waits for them, and re-layouts: 3.21 us -> 0.7 us
    broadcast_in_dim x3 -> x2, local copies, waits for them, and re-layouts: 0.12 us -> 2.28 us  [spread_rows(): everyone = jnp.broadcast_to(block[None], (count,) + block.shape)]
    reduce_sum x4 -> x0, other arithmetic: 2.11 us -> none  [the longest x2 1.08 us: norm_rows(): spread = jnp.mean(center * center, axis=-1, keepdims=True)]
  transfers between devices with their start and end apart: 0 -> 2, of which waited for: 0 -> 1; matrix products, arithmetic and copies ran while one was open for 0% -> 0% of each run, Pallas kernels for 0% -> 20%
where the time goes in v2:
time: 76.1 us; the launch traced here: 75.6 us
  blocking collectives  36 us (47%)
  Pallas kernels  25.4 us (33%)
  starting transfers between devices  7.39 us (10%)
  local copies, waits for them, and re-layouts  3.14 us (4%)
  waiting for transfers between devices  1.54 us (2%)
  matrix products  1.3 us (2%)
    pallas_call x1, Pallas kernels, project(): pl.pallas_call(project_kernel, grid=(rows // block,), in_specs=[tile, fix...  14.9 us
    all_to_all x1, blocking collectives, body(): lax.all_to_all(packed.reshape(count, lat_rows, width + LANES), 'page', 0,...  14.2 us
    all_to_all x1, blocking collectives, spread_pairs(): lax.all_to_all(everyone, 'page', 0, 0, axis_index_groups=sides, tiled=True)  11.2 us
    all_to_all x1, blocking collectives, spread_rows(): return lax.all_to_all(everyone, 'page', 0, 0, tiled=True)  10.5 us
    pallas_call x1, Pallas kernels, attend(): pl.pallas_call(attend_kernel, grid=(rows // block,), in_specs=[fixed((cou...  7.49 us
    all_to_all x1, starting transfers between devices, spread_rows(): return lax.all_to_all(everyone, 'page', 0, 0, tiled=True)  7.39 us
    pallas_call x1, Pallas kernels, mix(): pl.pallas_call(mix_kernel, out_shape=[jax.ShapeDtypeStruct((rows, width),...  3 us
    broadcast_in_dim x2, local copies, waits for them, and re-layouts, spread_rows(): everyone = jnp.broadcast_to(block[None], (count,) + block.shape)  2.28 us
  transfers between devices with their start and end apart: 2, of which 1 were waited for; matrix products, arithmetic and copies ran while one was open for 0% of the time, Pallas kernels for 20%

profile of v2, /device:TPU:0, one launch (start us, length us, event | category | flops | bytes accessed | tf_op | source)
XLA Modules:
  0.0 75.6 jit_solution(7860801617143428076)
XLA Ops:
  0.6 0.0 copy-start
  0.6 1.5 %broadcast_in_dim.6 = bf16[16,4,1024]{2,1,0:T(4,128)(2,1)} broadcast(bf16[4,1024]{1,0:T(4,128)(2,1)} %lat_ref.1), dimensions={1,2} | broadcast | bytes 139264 | tf_op jit(solution)/shard_map/broadcast_in_dim | solution.py:177
  2.2 7.4 %all-to-all-start = ((bf16[16,4,1024]{2,1,0:T(4,128)(2,1)}), bf16[16,4,1024]{2,1,0:T(4,128)(2,1)S(1)}, u32[]{:S(2)}, u32[]{:S(2)}) async-start(bf16[16,4,1024]{2,1,0:T(4,128)(2,1)} %broadcast_in_dim.6), calls=%async_computation | async-start | bytes 262144 | tf_op jit(solution)/shard_map/all_to_all | solution.py:178
  9.6 0.0 copy-start.2
  9.6 0.7 copy-done.2
  10.3 0.0 copy-start.1
  10.3 14.9 %project.1 = (bf16[2048,1024]{1,0:T(8,128)(2,1)}, bf16[2048,1024]{1,0:T(8,128)(2,1)}) custom-call(bf16[2048,1024]{1,0:T(8,128)(2,1)} %x_ref.1, f32[1,1024]{1,0:T(1,128)S(1)} %bitcast.19, bf16[1024,1024]{1,0:T(8,128)(2,1)} %wk_ref.1, bf16[1024,1024]{1,0:T(8,128)(2,1)} %wv_ref.1), custom_call_target="tpu_custom_call" | custom-call | flops 8589934592 | bytes 16777216 | tf_op jit(solution)/shard_map/project/pallas_call | solution.py:41
  25.1 0.0 all-to-all-done
  25.2 0.0 copy-done.1
  25.2 7.5 %attend.1 = bf16[64,1152]{1,0:T(8,128)(2,1)S(1)} custom-call(bf16[64,1024]{1,0:T(8,128)(2,1)S(1)} %reshape.31.lat_ref, f32[1,1024]{1,0:T(1,128)S(1)} %bitcast.18, bf16[1024,1024]{1,0:T(8,128)(2,1)} %wq_ref.1, bf16[2048,1024]{1,0:T(8,128)(2,1)} %get-tuple-element.6.k_ref, bf16[2048,1024]{1,0:T(8,128)(2,1)} %get-tuple-element.7.v_ref), custom_call_target="tpu_custom_call" | custom-call | flops 2147483648 | bytes 10485760 | tf_op jit(solution)/shard_map/attend/pallas_call | solution.py:121
  32.7 0.0 copy-start.3
  32.8 14.2 %all_to_all.20.parts_ref = bf16[16,4,1152]{2,1,0:T(4,128)(2,1)} all-to-all(bf16[16,4,1152]{2,1,0:T(4,128)(2,1)S(1)} %reshape.34), channel_id=1, replica_groups=mesh['slab'=2,'page'=16] {'page'}, dimensions={0} | all-to-all | bytes 294912 | tf_op jit(solution)/shard_map/all_to_all | solution.py:208
  47.0 3.0 %mix.1 = (bf16[4,1024]{1,0:T(4,128)(2,1)}, bf16[4,1024]{1,0:T(4,128)(2,1)}) custom-call(bf16[16,4,1152]{2,1,0:T(4,128)(2,1)} %all_to_all.20.parts_ref, bf16[4,1024]{1,0:T(4,128)(2,1)} %lat_ref.1, bf16[1024,1024]{1,0:T(8,128)(2,1)} %wo_ref.1, f32[1,1024]{1,0:T(1,128)} %bitcast.22), custom_call_target="tpu_custom_call" | custom-call | flops 8388608 | bytes 2244608 | tf_op jit(solution)/shard_map/mix/pallas_call | solution.py:164
  50.0 0.7 broadcast_in_dim.7
  50.7 10.5 %all_to_all.21 = bf16[16,4,1024]{2,1,0:T(4,128)(2,1)S(1)} all-to-all(bf16[16,4,1024]{2,1,0:T(4,128)(2,1)S(1)} %broadcast_in_dim.7), channel_id=1, replica_groups=mesh['slab'=2,'page'=16] {'page'}, dimensions={0} | all-to-all | bytes 262144 | tf_op jit(solution)/shard_map/all_to_all | solution.py:178
  61.3 0.0 copy-done.3
  61.3 0.2 fusion.7
  61.6 11.2 %all_to_all.22 = bf16[8,64,256]{2,1,0:T(8,128)(2,1)S(1)} all-to-all(bf16[8,64,256]{2,1,0:T(8,128)(2,1)S(1)} %broadcast_in_dim.8), channel_id=1, replica_groups={{0,2,4,6,8,10,12,14},{1,3,5,7,9,11,13,15},{16,18,20,22,24,26,28,30},{17..., dimensions={0} | all-to-all | bytes 524288 | tf_op jit(solution)/shard_map/all_to_all | solution.py:185
  72.8 0.0 collective-permute-start
  72.8 1.5 %collective-permute-done = bf16[8,64,256]{2,1,0:T(8,128)(2,1)S(1)} collective-permute-done((bf16[8,64,256]{2,1,0:T(8,128)(2,1)S(1)}, bf16[8,64,256]{2,1,0:T(8,128)(2,1)S(1)}, u32[]{:S(2)}, u32[]{:S(2)}) %collective-permute-start) | collective-permute-done | bytes 262176 | tf_op jit(solution)/shard_map/ppermute | solution.py:186
  74.4 0.1 pad_maximum_fusion
  74.5 0.0 copy-done
  74.5 1.1 %convolution_convert_fusion = bf16[64,256]{1,0:T(8,128)(2,1)} fusion(bf16[64,4096]{1,0:T(8,128)(2,1)S(1)} %bitcast.21, bf16[4096,256]{1,0:T(8,128)(2,1)S(1)} %copy-done), kind=kOutput, calls=%fused_computation | convolution fusion | flops 134234112 | bytes 2654208 | tf_op jit(solution)/shard_map/dot_general | solution.py:223
  (6 shorter events, 0.2 us)
Async XLA Ops:
  0.6 73.9 %copy-start = (bf16[4096,256]{1,0:T(8,128)(2,1)S(1)}, bf16[4096,256]{1,0:T(8,128)(2,1)}, u32[]{:S(2)}) copy-start(bf16[4096,256]{1,0:T(8,128)(2,1)} %param.21) | copy-start | bytes 6291460
  2.2 23.0 %all-to-all-start = ((bf16[16,4,1024]{2,1,0:T(4,128)(2,1)}), bf16[16,4,1024]{2,1,0:T(4,128)(2,1)S(1)}, u32[]{:S(2)}, u32[]{:S(2)}) async-start(bf16[16,4,1024]{2,1,0:T(4,128)(2,1)} %broadcast_in_dim.6), calls=%async_computation | async-start | bytes 262144 | tf_op jit(solution)/shard_map/all_to_all | solution.py:178
  9.6 0.7 copy-start.2
  10.3 14.9 %copy-start.1 = (f32[1024]{0:T(1024)S(1)}, f32[1024]{0:T(1024)}, u32[]{:S(2)}) copy-start(f32[1024]{0:T(1024)} %param.13) | copy-start | bytes 12292
  32.7 28.6 %copy-start.3 = (bf16[1024,256]{1,0:T(8,128)(2,1)S(1)}, bf16[1024,256]{1,0:T(8,128)(2,1)}, u32[]{:S(2)}) copy-start(bf16[1024,256]{1,0:T(8,128)(2,1)} %param.20) | copy-start | bytes 1572868
  72.8 1.5 %collective-permute-start = (bf16[8,64,256]{2,1,0:T(8,128)(2,1)S(1)}, bf16[8,64,256]{2,1,0:T(8,128)(2,1)S(1)}, u32[]{:S(2)}, u32[]{:S(2)}) collective-permute-start(bf16[8,64,256]{2,1,0:T(8,128)(2,1)S(1)} %all_to_all.22), channel_id=1, source_target_pairs={{0,1},{1,0},{2,3},{3,2},{4,5},{5,4},{6,7},{7,6},{8,9},{9,8},{10,11... | collective-permute-start | bytes 786440 | tf_op jit(solution)/shard_map/ppermute | solution.py:186

commit v3 on v2

--- a/solution.py
+++ b/solution.py
@@ -10,6 +10,7 @@
 HEADS = 16
 PACK = 4
 LANES = 128
+CHUNKS = 4
 MIB = 1024 * 1024
 
 
@@ -27,26 +28,76 @@
     return pl.BlockSpec(shape, lambda i: (0,) * len(shape), pipeline_mode=pl.Buffered(1))
 
 
-def project_kernel(x_ref, gain_ref, wk_ref, wv_ref, k_ref, v_ref):
-    x = x_ref[...].astype(jnp.float32)
-    pn = norm_rows(x, gain_ref[...]).astype(jnp.bfloat16)
-    k_ref[...] = jnp.dot(pn, wk_ref[...], preferred_element_type=jnp.float32).astype(jnp.bfloat16)
-    v_ref[...] = jnp.dot(pn, wv_ref[...], preferred_element_type=jnp.float32).astype(jnp.bfloat16)
+def project_kernel(
+    x_hbm, gain_ref, wk_hbm, wv_hbm, k_hbm, v_hbm, xs, wk, wv, ks, vs, pns, x_sem, w_sem, out_sem
+):
+    blocks, block, _ = xs.shape
+
+    def fetch(i):
+        return pltpu.make_async_copy(x_hbm.at[pl.ds(i * block, block)], xs.at[i], x_sem.at[i])
+
+    def put(src, dst, which, i):
+        return pltpu.make_async_copy(
+            src.at[i], dst.at[pl.ds(i * block, block)], out_sem.at[which, i]
+        )
+
+    def normed(i):
+        return norm_rows(xs[i].astype(jnp.float32), gain_ref[...]).astype(jnp.bfloat16)
+
+    def times(weight, i):
+        return jnp.dot(pns[i % 2], weight[...], preferred_element_type=jnp.float32).astype(
+            jnp.bfloat16
+        )
+
+    key_copy = pltpu.make_async_copy(wk_hbm, wk, w_sem.at[0])
+    value_copy = pltpu.make_async_copy(wv_hbm, wv, w_sem.at[1])
+    fetch(0).start()
+    key_copy.start()
+    for i in range(1, min(2, blocks)):
+        fetch(i).start()
+    value_copy.start()
+    for i in range(2, blocks):
+        fetch(i).start()
+    fetch(0).wait()
+    pns[0] = normed(0)
+    key_copy.wait()
+    for i in range(blocks):
+        ks[i] = times(wk, i)
+        put(ks, k_hbm, 0, i).start()
+        if i == 0:
+            value_copy.wait()
+        if i + 1 < blocks:
+            fetch(i + 1).wait()
+            pns[(i + 1) % 2] = normed(i + 1)
+        vs[i] = times(wv, i)
+        put(vs, v_hbm, 1, i).start()
+    for i in range(blocks):
+        put(ks, k_hbm, 0, i).wait()
+        put(vs, v_hbm, 1, i).wait()
 
 
 def project(patches, gain, w_key, w_value):
     rows, width = patches.shape
     block = math.gcd(rows, 512)
-    tile = pl.BlockSpec((block, width), lambda i: (i, 0))
+    blocks = rows // block
+    hbm = pl.BlockSpec(memory_space=pltpu.HBM)
     return pl.pallas_call(
         project_kernel,
-        grid=(rows // block,),
-        in_specs=[tile, fixed((1, width)), fixed((width, width)), fixed((width, width))],
-        out_specs=[tile, tile],
+        in_specs=[hbm, pl.BlockSpec(memory_space=pltpu.VMEM), hbm, hbm],
+        out_specs=[hbm, hbm],
         out_shape=[pltpu.HBM((rows, width), jnp.bfloat16)] * 2,
-        compiler_params=pltpu.CompilerParams(
-            dimension_semantics=("arbitrary",), vmem_limit_bytes=26 * MIB
-        ),
+        scratch_shapes=[
+            pltpu.VMEM((blocks, block, width), jnp.bfloat16),
+            pltpu.VMEM((width, width), jnp.bfloat16),
+            pltpu.VMEM((width, width), jnp.bfloat16),
+            pltpu.VMEM((blocks, block, width), jnp.bfloat16),
+            pltpu.VMEM((blocks, block, width), jnp.bfloat16),
+            pltpu.VMEM((2, block, width), jnp.bfloat16),
+            pltpu.SemaphoreType.DMA((blocks,)),
+            pltpu.SemaphoreType.DMA((2,)),
+            pltpu.SemaphoreType.DMA((2, blocks)),
+        ],
+        compiler_params=pltpu.CompilerParams(vmem_limit_bytes=32 * MIB),
         cost_estimate=pl.CostEstimate(
             flops=4 * rows * width * width,
             transcendentals=rows,
@@ -56,10 +107,10 @@
     )(in_hbm(patches), gain.reshape(1, width), in_hbm(w_key), in_hbm(w_value))
 
 
-def attend_kernel(lat_ref, gain_ref, wq_ref, k_ref, v_ref, out_ref, qbd, acc, dacc):
+def attend_kernel(q_ref, k_ref, v_ref, out_ref, qbd, acc, dacc):
     step = pl.program_id(0)
     block = k_ref.shape[0]
-    latents, width = lat_ref.shape
+    latents, width = q_ref.shape
     head_dim = width // HEADS
     span = PACK * head_dim
     groups = HEADS // PACK
@@ -69,14 +120,12 @@
     def _():
         acc[...] = jnp.zeros_like(acc)
         dacc[...] = jnp.zeros_like(dacc)
-        lat_norm = norm_rows(lat_ref[...].astype(jnp.float32), gain_ref[...]).astype(jnp.bfloat16)
-        query = jnp.dot(lat_norm, wq_ref[...], preferred_element_type=jnp.float32)
         for g in range(groups):
-            part = query[:, g * span : (g + 1) * span]
+            part = q_ref[:, g * span : (g + 1) * span]
             for h in range(PACK):
                 qbd[g, h * latents : (h + 1) * latents, :] = jnp.where(
                     lane_head == h, part, jnp.zeros_like(part)
-                ).astype(jnp.bfloat16)
+                )
 
     factor = math.log2(math.e) / math.sqrt(head_dim)
     for g in range(groups):
@@ -111,9 +160,9 @@
         out_ref[:, width:] = out.astype(jnp.bfloat16)
 
 
-def attend(latents, gain, w_query, keys, values):
+def attend(query, keys, values):
     rows, width = keys.shape
-    count = latents.shape[0]
+    count = query.shape[0]
     block = math.gcd(rows, 512)
     span = PACK * (width // HEADS)
     groups = HEADS // PACK
@@ -121,7 +170,7 @@
     return pl.pallas_call(
         attend_kernel,
         grid=(rows // block,),
-        in_specs=[fixed((count, width)), fixed((1, width)), fixed((width, width)), tile, tile],
+        in_specs=[fixed((count, width)), tile, tile],
         out_specs=pl.BlockSpec((count, width + LANES), lambda i: (0, 0)),
         out_shape=jax.ShapeDtypeStruct((count, width + LANES), jnp.bfloat16),
         scratch_shapes=[
@@ -130,20 +179,71 @@
             pltpu.VMEM((groups, PACK * count, LANES), jnp.float32),
         ],
         compiler_params=pltpu.CompilerParams(
-            dimension_semantics=("arbitrary",), vmem_limit_bytes=44 * MIB
+            dimension_semantics=("arbitrary",), vmem_limit_bytes=30 * MIB
         ),
         cost_estimate=pl.CostEstimate(
             flops=4 * rows * count * PACK * width,
             transcendentals=rows * count * HEADS,
-            bytes_accessed=4 * rows * width + 2 * width * width,
+            bytes_accessed=4 * rows * width,
         ),
         name="attend",
-    )(latents, gain.reshape(1, width), in_hbm(w_query), in_hbm(keys), in_hbm(values))
-
-
-def mix_kernel(parts_ref, lat_ref, wo_ref, gain_ref, res_ref, mlp_ref):
+    )(query, in_hbm(keys), in_hbm(values))
+
+
+def start_chunks(hbm, chunks, sem):
+    size = chunks.shape[1]
+    fetches = [
+        pltpu.make_async_copy(hbm.at[pl.ds(i * size, size)], chunks.at[i], sem.at[i])
+        for i in range(chunks.shape[0])
+    ]
+    for fetch in fetches:
+        fetch.start()
+    return fetches
+
+
+def times_chunks(rows, fetches, chunks, total):
+    size = chunks.shape[1]
+    for i, fetch in enumerate(fetches):
+        fetch.wait()
+        part = jnp.dot(
+            rows[:, i * size : (i + 1) * size], chunks[i], preferred_element_type=jnp.float32
+        )
+        total = part if total is None else total + part
+    return total
+
+
+def ask_kernel(lat_ref, wq_hbm, gain_ref, out_ref, wq, sem):
+    fetches = start_chunks(wq_hbm, wq, sem)
+    lat_norm = norm_rows(lat_ref[...].astype(jnp.float32), gain_ref[...]).astype(jnp.bfloat16)
+    query = times_chunks(lat_norm, fetches, wq, None).astype(jnp.bfloat16)
+    for j in range(out_ref.shape[0]):
+        out_ref[j] = query
+
+
+def ask(latents, w_query, gain, count):
+    rows, width = latents.shape
+    vmem = pl.BlockSpec(memory_space=pltpu.VMEM)
+    return pl.pallas_call(
+        ask_kernel,
+        in_specs=[vmem, pl.BlockSpec(memory_space=pltpu.HBM), vmem],
+        out_shape=jax.ShapeDtypeStruct((count, rows, width), jnp.bfloat16),
+        scratch_shapes=[
+            pltpu.VMEM((CHUNKS, width // CHUNKS, width), jnp.bfloat16),
+            pltpu.SemaphoreType.DMA((CHUNKS,)),
+        ],
+        cost_estimate=pl.CostEstimate(
+            flops=2 * rows * width * width,
+            transcendentals=rows,
+            bytes_accessed=2 * width * width + 2 * (count + 1) * rows * width,
+        ),
+        name="ask",
+    )(latents, in_hbm(w_query), gain.reshape(1, width))
+
+
+def mix_kernel(parts_ref, lat_ref, wo_hbm, gain_ref, res_ref, mlp_ref, wo, sem):
     rows, width = lat_ref.shape
     head_dim = width // HEADS
+    fetches = start_chunks(wo_hbm, wo, sem)
     total = parts_ref[0].astype(jnp.float32)
     for j in range(1, parts_ref.shape[0]):
         total = total + parts_ref[j].astype(jnp.float32)
@@ -152,30 +252,38 @@
         [jnp.broadcast_to(denom[:, h : h + 1], (rows, head_dim)) for h in range(HEADS)], axis=1
     )
     attended = (total[:, :width] / wide).astype(jnp.bfloat16)
-    mixed = lat_ref[...].astype(jnp.float32) + jnp.dot(
-        attended, wo_ref[...], preferred_element_type=jnp.float32
-    )
+    mixed = times_chunks(attended, fetches, wo, lat_ref[...].astype(jnp.float32))
     res_ref[...] = mixed.astype(jnp.bfloat16)
-    mlp_ref[...] = norm_rows(mixed, gain_ref[...]).astype(jnp.bfloat16)
+    mlp_in = norm_rows(mixed, gain_ref[...]).astype(jnp.bfloat16)
+    for j in range(mlp_ref.shape[0]):
+        mlp_ref[j] = mlp_in
 
 
 def mix(parts, latents, w_out, gain):
     rows, width = latents.shape
+    vmem = pl.BlockSpec(memory_space=pltpu.VMEM)
     return pl.pallas_call(
         mix_kernel,
-        out_shape=[jax.ShapeDtypeStruct((rows, width), jnp.bfloat16)] * 2,
+        in_specs=[vmem, vmem, pl.BlockSpec(memory_space=pltpu.HBM), vmem],
+        out_shape=[
+            jax.ShapeDtypeStruct((rows, width), jnp.bfloat16),
+            jax.ShapeDtypeStruct((parts.shape[0], rows, width), jnp.bfloat16),
+        ],
+        scratch_shapes=[
+            pltpu.VMEM((CHUNKS, width // CHUNKS, width), jnp.bfloat16),
+            pltpu.SemaphoreType.DMA((CHUNKS,)),
+        ],
         cost_estimate=pl.CostEstimate(
             flops=2 * rows * width * width,
             transcendentals=rows,
             bytes_accessed=2 * width * width + 2 * parts.size,
         ),
         name="mix",
-    )(parts, latents, w_out, gain.reshape(1, width))
-
-
-def spread_rows(block, count):
-    everyone = jnp.broadcast_to(block[None], (count,) + block.shape)
-    return lax.all_to_all(everyone, "page", 0, 0, tiled=True)
+    )(parts, latents, in_hbm(w_out), gain.reshape(1, width))
+
+
+def exchange(blocks):
+    return lax.all_to_all(blocks, "page", 0, 0, tiled=True)
 
 
 def spread_pairs(block, count):
@@ -202,14 +310,12 @@
 ):
     count = lax.axis_size("page")
     lat_rows, width = latents.shape
-    lat_all = spread_rows(latents, count).reshape(count * lat_rows, width)
+    query = exchange(ask(latents, w_query, lat_gain, count)).reshape(count * lat_rows, width)
     keys, values = project(patches, patch_gain, w_key, w_value)
-    packed = attend(lat_all, lat_gain, w_query, keys, values)
-    parts = lax.all_to_all(
-        packed.reshape(count, lat_rows, width + LANES), "page", 0, 0, tiled=True
-    )
+    packed = attend(query, keys, values)
+    parts = exchange(packed.reshape(count, lat_rows, width + LANES))
     resampled, mlp_in = mix(parts, latents, w_out, mlp_gain)
-    mlp_all = spread_rows(mlp_in, count).reshape(count * lat_rows, width)
+    mlp_all = exchange(mlp_in).reshape(count * lat_rows, width)
     hidden = jax.nn.gelu(
         jnp.dot(mlp_all, w_hidden, preferred_element_type=jnp.float32), approximate=True
     ).astype(jnp.bfloat16)

time: 76.1 us -> 74.6 us (0.980)
  local copies, waits for them, and re-layouts: 3.14 us -> 0.18 us
  blocking collectives: 36 us -> 36.9 us
    broadcast_in_dim x2 -> x0, local copies, waits for them, and re-layouts: 2.28 us -> none  [spread_rows(): everyone = jnp.broadcast_to(block[None], (count,) + block.shape)]
    pallas_call x2 -> x3, Pallas kernels: 17.9 us -> 19.8 us  [the longest x1 12.9 us: project(): pl.pallas_call(project_kernel, in_specs=[hbm, pl.BlockSpec(memory_space=p...]
    pallas_call x1, Pallas kernels: 7.49 us -> 6.2 us  [attend(): pl.pallas_call(attend_kernel, grid=(rows // block,), in_specs=[fixed((cou...]
    all_to_all x2, blocking collectives: 24.8 us -> 25.6 us  [exchange(): return lax.all_to_all(blocks, 'page', 0, 0, tiled=True)]
  transfers between devices with their start and end apart: 2 -> 2, of which waited for: 1 -> 1; matrix products, arithmetic and copies ran while one was open for 0% -> 0% of each run, Pallas kernels for 20% -> 17%
where the time goes in v3:
time: 74.6 us; the launch traced here: 74.2 us
  blocking collectives  36.9 us (49%)
  Pallas kernels  26 us (35%)
  starting transfers between devices  7.4 us (10%)
  waiting for transfers between devices  1.54 us (2%)
  matrix products  1.3 us (2%)
  between operations  0.77 us (1%)
    all_to_all x2, blocking collectives, exchange(): return lax.all_to_all(blocks, 'page', 0, 0, tiled=True)  25.6 us
    pallas_call x1, Pallas kernels, project(): pl.pallas_call(project_kernel, in_specs=[hbm, pl.BlockSpec(memory_space=p...  12.9 us
    all_to_all x1, blocking collectives, spread_pairs(): lax.all_to_all(everyone, 'page', 0, 0, axis_index_groups=sides, tiled=True)  11.2 us
    all_to_all x1, starting transfers between devices, exchange(): return lax.all_to_all(blocks, 'page', 0, 0, tiled=True)  7.4 us
    pallas_call x1, Pallas kernels, attend(): pl.pallas_call(attend_kernel, grid=(rows // block,), in_specs=[fixed((cou...  6.2 us
    pallas_call x1, Pallas kernels, mix(): pl.pallas_call(mix_kernel, in_specs=[vmem, vmem, pl.BlockSpec(memory_spac...  3.59 us
    pallas_call x1, Pallas kernels, ask(): pl.pallas_call(ask_kernel, in_specs=[vmem, pl.BlockSpec(memory_space=pltp...  3.26 us
    ppermute x1, waiting for transfers between devices, spread_pairs(): theirs = lax.ppermute(mine, 'page', [(i, i ^ 1) for i in range(count)])  1.53 us
  transfers between devices with their start and end apart: 2, of which 1 were waited for; matrix products, arithmetic and copies ran while one was open for 0% of the time, Pallas kernels for 17%

profile of v3, /device:TPU:0, one launch (start us, length us, event | category | flops | bytes accessed | tf_op | source)
XLA Modules:
  0.0 74.2 jit_solution(2301247232123977512)
XLA Ops:
  0.6 0.0 copy-start
  0.6 0.0 copy-start.1
  0.7 3.3 %ask.1 = bf16[16,4,1024]{2,1,0:T(4,128)(2,1)} custom-call(bf16[4,1024]{1,0:T(4,128)(2,1)} %lat_ref.3, bf16[1024,1024]{1,0:T(8,128)(2,1)} %wq_hbm.1, f32[1,1024]{1,0:T(1,128)} %bitcast.21), custom_call_target="tpu_custom_call" | custom-call | flops 8388608 | bytes 2236416 | tf_op jit(solution)/shard_map/ask/pallas_call | solution.py:226
  3.9 7.4 %all-to-all-start = ((bf16[16,4,1024]{2,1,0:T(4,128)(2,1)}), bf16[16,4,1024]{2,1,0:T(4,128)(2,1)S(1)}, u32[]{:S(2)}, u32[]{:S(2)}) async-start(bf16[16,4,1024]{2,1,0:T(4,128)(2,1)} %ask.1), calls=%async_computation | async-start | bytes 262144 | tf_op jit(solution)/shard_map/all_to_all | solution.py:286
  11.3 0.0 copy-done.1
  11.3 12.9 %project.1 = (bf16[2048,1024]{1,0:T(8,128)(2,1)}, bf16[2048,1024]{1,0:T(8,128)(2,1)}) custom-call(bf16[2048,1024]{1,0:T(8,128)(2,1)} %x_hbm.1, f32[1,1024]{1,0:T(1,128)S(1)} %bitcast.18, bf16[1024,1024]{1,0:T(8,128)(2,1)} %wk_hbm.1, bf16[1024,1024]{1,0:T(8,128)(2,1)} %wv_hbm.1), custom_call_target="tpu_custom_call" | custom-call | flops 8589934592 | bytes 16777216 | tf_op jit(solution)/shard_map/project/pallas_call | solution.py:84
  24.3 0.0 all-to-all-done
  24.3 6.2 %attend.1 = bf16[64,1152]{1,0:T(8,128)(2,1)S(1)} custom-call(bf16[64,1024]{1,0:T(8,128)(2,1)S(1)} %reshape.30.q_ref, bf16[2048,1024]{1,0:T(8,128)(2,1)} %get-tuple-element.6.k_ref, bf16[2048,1024]{1,0:T(8,128)(2,1)} %get-tuple-element.7.v_ref), custom_call_target="tpu_custom_call" | custom-call | flops 2147483648 | bytes 8388608 | tf_op jit(solution)/shard_map/attend/pallas_call | solution.py:170
  30.5 0.0 copy-start.2
  30.6 14.2 %all_to_all.20.parts_ref = bf16[16,4,1152]{2,1,0:T(4,128)(2,1)} all-to-all(bf16[16,4,1152]{2,1,0:T(4,128)(2,1)S(1)} %reshape.32), channel_id=1, replica_groups=mesh['slab'=2,'page'=16] {'page'}, dimensions={0} | all-to-all | bytes 294912 | tf_op jit(solution)/shard_map/all_to_all | solution.py:286
  44.8 3.6 %mix.1 = (bf16[4,1024]{1,0:T(4,128)(2,1)}, bf16[16,4,1024]{2,1,0:T(4,128)(2,1)}) custom-call(bf16[16,4,1152]{2,1,0:T(4,128)(2,1)} %all_to_all.20.parts_ref, bf16[4,1024]{1,0:T(4,128)(2,1)} %lat_ref.3, bf16[1024,1024]{1,0:T(8,128)(2,1)} %wo_hbm.1, f32[1,1024]{1,0:T(1,128)} %bitcast.22), custom_call_target="tpu_custom_call" | custom-call | flops 8388608 | bytes 2244608 | tf_op jit(solution)/shard_map/mix/pallas_call | solution.py:265
  48.4 11.4 %all_to_all.21 = bf16[16,4,1024]{2,1,0:T(4,128)(2,1)S(1)} all-to-all(bf16[16,4,1024]{2,1,0:T(4,128)(2,1)} %get-tuple-element.9), channel_id=1, replica_groups=mesh['slab'=2,'page'=16] {'page'}, dimensions={0} | all-to-all | bytes 262144 | tf_op jit(solution)/shard_map/all_to_all | solution.py:286
  59.9 0.0 copy-done.2
  59.9 0.2 fusion.7
  60.1 11.2 %all_to_all.22 = bf16[8,64,256]{2,1,0:T(8,128)(2,1)S(1)} all-to-all(bf16[8,64,256]{2,1,0:T(8,128)(2,1)S(1)} %broadcast_in_dim.2), channel_id=1, replica_groups={{0,2,4,6,8,10,12,14},{1,3,5,7,9,11,13,15},{16,18,20,22,24,26,28,30},{17..., dimensions={0} | all-to-all | bytes 524288 | tf_op jit(solution)/shard_map/all_to_all | solution.py:293
  71.4 0.0 collective-permute-start
  71.4 1.5 %collective-permute-done = bf16[8,64,256]{2,1,0:T(8,128)(2,1)S(1)} collective-permute-done((bf16[8,64,256]{2,1,0:T(8,128)(2,1)S(1)}, bf16[8,64,256]{2,1,0:T(8,128)(2,1)S(1)}, u32[]{:S(2)}, u32[]{:S(2)}) %collective-permute-start) | collective-permute-done | bytes 262176 | tf_op jit(solution)/shard_map/ppermute | solution.py:294
  73.0 0.1 pad_maximum_fusion
  73.1 0.0 copy-done
  73.1 1.1 %convolution_convert_fusion = bf16[64,256]{1,0:T(8,128)(2,1)} fusion(bf16[64,4096]{1,0:T(8,128)(2,1)S(1)} %bitcast.20, bf16[4096,256]{1,0:T(8,128)(2,1)S(1)} %copy-done), kind=kOutput, calls=%fused_computation | convolution fusion | flops 134234112 | bytes 2654208 | tf_op jit(solution)/shard_map/dot_general | solution.py:329
  (6 shorter events, 0.2 us)
Async XLA Ops:
  0.6 72.4 %copy-start = (bf16[4096,256]{1,0:T(8,128)(2,1)S(1)}, bf16[4096,256]{1,0:T(8,128)(2,1)}, u32[]{:S(2)}) copy-start(bf16[4096,256]{1,0:T(8,128)(2,1)} %param.21) | copy-start | bytes 6291460
  0.6 10.7 %copy-start.1 = (f32[1024]{0:T(1024)S(1)}, f32[1024]{0:T(1024)}, u32[]{:S(2)}) copy-start(f32[1024]{0:T(1024)} %param.14) | copy-start | bytes 12292
  3.9 20.3 %all-to-all-start = ((bf16[16,4,1024]{2,1,0:T(4,128)(2,1)}), bf16[16,4,1024]{2,1,0:T(4,128)(2,1)S(1)}, u32[]{:S(2)}, u32[]{:S(2)}) async-start(bf16[16,4,1024]{2,1,0:T(4,128)(2,1)} %ask.1), calls=%async_computation | async-start | bytes 262144 | tf_op jit(solution)/shard_map/all_to_all | solution.py:286
  30.5 29.3 %copy-start.2 = (bf16[1024,256]{1,0:T(8,128)(2,1)S(1)}, bf16[1024,256]{1,0:T(8,128)(2,1)}, u32[]{:S(2)}) copy-start(bf16[1024,256]{1,0:T(8,128)(2,1)} %param.20) | copy-start | bytes 1572868
  71.4 1.5 %collective-permute-start = (bf16[8,64,256]{2,1,0:T(8,128)(2,1)S(1)}, bf16[8,64,256]{2,1,0:T(8,128)(2,1)S(1)}, u32[]{:S(2)}, u32[]{:S(2)}) collective-permute-start(bf16[8,64,256]{2,1,0:T(8,128)(2,1)S(1)} %all_to_all.22), channel_id=1, source_target_pairs={{0,1},{1,0},{2,3},{3,2},{4,5},{5,4},{6,7},{7,6},{8,9},{9,8},{10,11... | collective-permute-start | bytes 786440 | tf_op jit(solution)/shard_map/ppermute | solution.py:294

commit v4 on v3

--- a/solution.py
+++ b/solution.py
@@ -240,59 +240,24 @@
     )(latents, in_hbm(w_query), gain.reshape(1, width))
 
 
-def mix_kernel(parts_ref, lat_ref, wo_hbm, gain_ref, res_ref, mlp_ref, wo, sem):
-    rows, width = lat_ref.shape
-    head_dim = width // HEADS
-    fetches = start_chunks(wo_hbm, wo, sem)
-    total = parts_ref[0].astype(jnp.float32)
-    for j in range(1, parts_ref.shape[0]):
-        total = total + parts_ref[j].astype(jnp.float32)
-    denom = total[:, width : width + HEADS] + total[:, width + HEADS : width + 2 * HEADS]
-    wide = jnp.concatenate(
-        [jnp.broadcast_to(denom[:, h : h + 1], (rows, head_dim)) for h in range(HEADS)], axis=1
-    )
-    attended = (total[:, :width] / wide).astype(jnp.bfloat16)
-    mixed = times_chunks(attended, fetches, wo, lat_ref[...].astype(jnp.float32))
-    res_ref[...] = mixed.astype(jnp.bfloat16)
-    mlp_in = norm_rows(mixed, gain_ref[...]).astype(jnp.bfloat16)
-    for j in range(mlp_ref.shape[0]):
-        mlp_ref[j] = mlp_in
-
-
-def mix(parts, latents, w_out, gain):
-    rows, width = latents.shape
-    vmem = pl.BlockSpec(memory_space=pltpu.VMEM)
-    return pl.pallas_call(
-        mix_kernel,
-        in_specs=[vmem, vmem, pl.BlockSpec(memory_space=pltpu.HBM), vmem],
-        out_shape=[
-            jax.ShapeDtypeStruct((rows, width), jnp.bfloat16),
-            jax.ShapeDtypeStruct((parts.shape[0], rows, width), jnp.bfloat16),
-        ],
-        scratch_shapes=[
-            pltpu.VMEM((CHUNKS, width // CHUNKS, width), jnp.bfloat16),
-            pltpu.SemaphoreType.DMA((CHUNKS,)),
-        ],
-        cost_estimate=pl.CostEstimate(
-            flops=2 * rows * width * width,
-            transcendentals=rows,
-            bytes_accessed=2 * width * width + 2 * parts.size,
-        ),
-        name="mix",
-    )(parts, latents, in_hbm(w_out), gain.reshape(1, width))
-
-
 def exchange(blocks):
     return lax.all_to_all(blocks, "page", 0, 0, tiled=True)
 
 
-def spread_pairs(block, count):
-    chips = count // 2
-    sides = [[2 * chip + side for chip in range(chips)] for side in range(2)]
-    everyone = jnp.broadcast_to(block[None], (chips,) + block.shape)
-    mine = lax.all_to_all(everyone, "page", 0, 0, axis_index_groups=sides, tiled=True)
+def spread(block, count):
+    return jnp.broadcast_to(block[None], (count,) + block.shape)
+
+
+def exchange_side(blocks, count):
+    sides = [[2 * chip + side for chip in range(count // 2)] for side in range(2)]
+    return lax.all_to_all(blocks, "page", 0, 0, axis_index_groups=sides, tiled=True)
+
+
+def join_sides(mine, count):
     theirs = lax.ppermute(mine, "page", [(i, i ^ 1) for i in range(count)])
-    return mine, theirs
+    even = lax.axis_index("page") % 2 == 0
+    both = jnp.stack([jnp.where(even, mine, theirs), jnp.where(even, theirs, mine)], axis=1)
+    return both.reshape((count,) + mine.shape[1:])
 
 
 def body(
@@ -310,22 +275,31 @@
 ):
     count = lax.axis_size("page")
     lat_rows, width = latents.shape
-    query = exchange(ask(latents, w_query, lat_gain, count)).reshape(count * lat_rows, width)
+    query_side = exchange_side(ask(latents, w_query, lat_gain, count // 2), count)
     keys, values = project(patches, patch_gain, w_key, w_value)
+    query_side, keys, values = lax.optimization_barrier((query_side, keys, values))
+    query = join_sides(query_side, count).reshape(count * lat_rows, width)
     packed = attend(query, keys, values)
     parts = exchange(packed.reshape(count, lat_rows, width + LANES))
-    resampled, mlp_in = mix(parts, latents, w_out, mlp_gain)
-    mlp_all = exchange(mlp_in).reshape(count * lat_rows, width)
+    summed = jnp.sum(parts.astype(jnp.float32), axis=0)
+    denom = summed[:, width : width + HEADS] + summed[:, width + HEADS : width + 2 * HEADS]
+    attended = (
+        (summed[:, :width].reshape(lat_rows, HEADS, width // HEADS) / denom[:, :, None])
+        .reshape(lat_rows, width)
+        .astype(jnp.bfloat16)
+    )
+    mixed = latents.astype(jnp.float32) + jnp.dot(
+        attended, w_out, preferred_element_type=jnp.float32
+    )
+    resampled = mixed.astype(jnp.bfloat16)
+    mlp_in = norm_rows(mixed, mlp_gain).astype(jnp.bfloat16)
+    mlp_all = exchange(spread(mlp_in, count)).reshape(count * lat_rows, width)
     hidden = jax.nn.gelu(
         jnp.dot(mlp_all, w_hidden, preferred_element_type=jnp.float32), approximate=True
     ).astype(jnp.bfloat16)
     rows, units = hidden.shape
-    mine, theirs = spread_pairs(hidden, count)
-    even = lax.axis_index("page") % 2 == 0
-    both = jnp.stack([jnp.where(even, mine, theirs), jnp.where(even, theirs, mine)], axis=1)
-    hidden_all = jnp.transpose(both.reshape(count, rows, units), (1, 0, 2)).reshape(
-        rows, count * units
-    )
+    hidden_all = join_sides(exchange_side(spread(hidden, count // 2), count), count)
+    hidden_all = jnp.transpose(hidden_all, (1, 0, 2)).reshape(rows, count * units)
     connector = jnp.dot(hidden_all, w_connect, preferred_element_type=jnp.float32).astype(
         jnp.bfloat16
     )

time: 74.6 us -> 74.7 us (level)
  Pallas kernels: 26 us -> 22.3 us
  matrix products: 1.3 us -> 3.39 us
  waiting for transfers between devices: 1.54 us -> 2.76 us
  other arithmetic: 0.09 us -> 1.21 us
  blocking collectives: 36.9 us -> 36 us
    pallas_call x1 -> x0, Pallas kernels: 3.59 us -> none  [mix(): pl.pallas_call(mix_kernel, in_specs=[vmem, vmem, pl.BlockSpec(memory_spac...]
    dot_general x0 -> x1, matrix products: none -> 2.09 us  [body(): jnp.dot(attended, w_out, preferred_element_type=jnp.float32)]
    ppermute x1 -> x2, waiting for transfers between devices: 1.53 us -> 2.76 us  [join_sides(): theirs = lax.ppermute(mine, 'page', [(i, i ^ 1) for i in range(count)])]
    all_to_all x2, blocking collectives: 25.6 us -> 24.7 us  [exchange(): return lax.all_to_all(blocks, 'page', 0, 0, tiled=True)]
  transfers between devices with their start and end apart: 2 -> 3, of which waited for: 1 -> 2; matrix products, arithmetic and copies ran while one was open for 0% -> 0% of each run, Pallas kernels for 17% -> 17%
where the time goes in v4:
time: 74.7 us; the launch traced here: 74.3 us
  blocking collectives  36 us (48%)
  Pallas kernels  22.3 us (30%)
  starting transfers between devices  7.37 us (10%)
  matrix products  3.39 us (5%)
  waiting for transfers between devices  2.76 us (4%)
  other arithmetic  1.21 us (2%)
  between operations  0.83 us (1%)
    all_to_all x2, blocking collectives, exchange(): return lax.all_to_all(blocks, 'page', 0, 0, tiled=True)  24.7 us
    pallas_call x1, Pallas kernels, project(): pl.pallas_call(project_kernel, in_specs=[hbm, pl.BlockSpec(memory_space=p...  12.9 us
    all_to_all x1, blocking collectives, exchange_side(): lax.all_to_all(blocks, 'page', 0, 0, axis_index_groups=sides, tiled=True)  11.2 us
    all_to_all x1, starting transfers between devices, exchange_side(): lax.all_to_all(blocks, 'page', 0, 0, axis_index_groups=sides, tiled=True)  7.29 us
    pallas_call x1, Pallas kernels, attend(): pl.pallas_call(attend_kernel, grid=(rows // block,), in_specs=[fixed((cou...  6.2 us
    pallas_call x1, Pallas kernels, ask(): pl.pallas_call(ask_kernel, in_specs=[vmem, pl.BlockSpec(memory_space=pltp...  3.21 us
    ppermute x2, waiting for transfers between devices, join_sides(): theirs = lax.ppermute(mine, 'page', [(i, i ^ 1) for i in range(count)])  2.76 us
    dot_general x1, matrix products, body(): jnp.dot(attended, w_out, preferred_element_type=jnp.float32)  2.09 us
  transfers between devices with their start and end apart: 3, of which 2 were waited for; matrix products, arithmetic and copies ran while one was open for 0% of the time, Pallas kernels for 17%

profile of v4, /device:TPU:0, one launch (start us, length us, event | category | flops | bytes accessed | tf_op | source)
XLA Modules:
  0.0 74.3 jit_solution(15740878359439036723)
XLA Ops:
  0.6 0.0 copy-start
  0.6 0.0 copy-start.1
  0.7 3.2 %ask.1 = bf16[8,4,1024]{2,1,0:T(4,128)(2,1)} custom-call(bf16[4,1024]{1,0:T(4,128)(2,1)} %lat_ref.1, bf16[1024,1024]{1,0:T(8,128)(2,1)} %wq_hbm.1, f32[1,1024]{1,0:T(1,128)} %bitcast.25), custom_call_target="tpu_custom_call" | custom-call | flops 8388608 | bytes 2170880 | tf_op jit(solution)/shard_map/ask/pallas_call | solution.py:226
  3.9 7.3 %all-to-all-start = ((bf16[8,4,1024]{2,1,0:T(4,128)(2,1)}), bf16[8,4,1024]{2,1,0:T(4,128)(2,1)S(1)}, u32[]{:S(2)}, u32[]{:S(2)}) async-start(bf16[8,4,1024]{2,1,0:T(4,128)(2,1)} %ask.1), calls=%async_computation | async-start | bytes 131072 | tf_op jit(solution)/shard_map/all_to_all | solution.py:253
  11.2 0.0 copy-done.1
  11.2 12.9 %project.1 = (bf16[2048,1024]{1,0:T(8,128)(2,1)}, bf16[2048,1024]{1,0:T(8,128)(2,1)}) custom-call(bf16[2048,1024]{1,0:T(8,128)(2,1)} %x_hbm.1, f32[1,1024]{1,0:T(1,128)S(1)} %bitcast.22, bf16[1024,1024]{1,0:T(8,128)(2,1)} %wk_hbm.1, bf16[1024,1024]{1,0:T(8,128)(2,1)} %wv_hbm.1), custom_call_target="tpu_custom_call" | custom-call | flops 8589934592 | bytes 16777216 | tf_op jit(solution)/shard_map/project/pallas_call | solution.py:84
  24.1 0.0 all-to-all-done
  24.1 0.1 collective-permute-start
  24.2 1.2 %collective-permute-done = bf16[8,4,1024]{2,1,0:T(4,128)(2,1)S(1)} collective-permute-done((bf16[8,4,1024]{2,1,0:T(4,128)(2,1)S(1)}, bf16[8,4,1024]{2,1,0:T(4,128)(2,1)S(1)}, u32[]{:S(2)}, u32[]{:S(2)}) %collective-permute-start) | collective-permute-done | bytes 65568 | tf_op jit(solution)/shard_map/ppermute | solution.py:257
  25.4 0.1 select_bitcast_fusion.3
  25.5 0.1 pad_maximum_fusion.1
  25.7 0.0 copy-start.3
  25.7 6.2 %attend.1 = bf16[64,1152]{1,0:T(8,128)(2,1)S(1)} custom-call(bf16[64,1024]{1,0:T(8,128)(2,1)S(1)} %reshape_reshape.3.q_ref, bf16[2048,1024]{1,0:T(8,128)(2,1)} %get-tuple-element.10.k_ref, bf16[2048,1024]{1,0:T(8,128)(2,1)} %get-tuple-element.11.v_ref), custom_call_target="tpu_custom_call" | custom-call | flops 2147483648 | bytes 8388608 | tf_op jit(solution)/shard_map/attend/pallas_call | solution.py:170
  31.9 0.0 copy-start.4
  31.9 0.0 copy-start.2
  32.0 14.2 %all_to_all.20 = bf16[16,4,1152]{2,1,0:T(4,128)(2,1)S(1)} all-to-all(bf16[16,4,1152]{2,1,0:T(4,128)(2,1)S(1)} %reshape.43), channel_id=1, replica_groups=mesh['slab'=2,'page'=16] {'page'}, dimensions={0} | all-to-all | bytes 294912 | tf_op jit(solution)/shard_map/all_to_all | solution.py:244
  46.2 0.1 convert_reduce_fusion
  46.3 0.1 slice_add_fusion
  46.3 0.1 div.17
  46.4 0.1 div.18
  46.5 0.0 copy-done.3
  46.5 2.1 %fusion.10 = (f32[4]{0:T(128)S(1)}, f32[4,1024]{1,0:T(4,128)S(1)}) fusion(bf16[1024,1024]{1,0:T(8,128)(2,1)} %param.19, f32[4,1024]{1,0:T(4,128)S(1)} %div.18, f32[4,1152]{1,0:T(4,128)S(1)} %convert_reduce_fusion, bf16[4,1024]{1,0:T(4,128)(2,1)S(1)} %copy-done.3), kind=kOutput, calls=%fused_computation.25 | convolution fusion | flops 8409084 | bytes 2154512 | tf_op jit(solution)/shard_map/dot_general | solution.py:291
  48.6 0.2 multiply_reduce_fusion
  48.8 0.0 copy-done.4
  48.8 0.6 multiply_convert_fusion
  49.5 10.5 %all_to_all.21 = bf16[16,4,1024]{2,1,0:T(4,128)(2,1)S(1)} all-to-all(bf16[16,4,1024]{2,1,0:T(4,128)(2,1)S(1)} %broadcast_in_dim.4), channel_id=1, replica_groups=mesh['slab'=2,'page'=16] {'page'}, dimensions={0} | all-to-all | bytes 262144 | tf_op jit(solution)/shard_map/all_to_all | solution.py:244
  60.0 0.2 fusion.7
  60.3 11.2 %all_to_all.22 = bf16[8,64,256]{2,1,0:T(8,128)(2,1)S(1)} all-to-all(bf16[8,64,256]{2,1,0:T(8,128)(2,1)S(1)} %broadcast_in_dim.5), channel_id=1, replica_groups={{0,2,4,6,8,10,12,14},{1,3,5,7,9,11,13,15},{16,18,20,22,24,26,28,30},{17..., dimensions={0} | all-to-all | bytes 524288 | tf_op jit(solution)/shard_map/all_to_all | solution.py:253
  71.5 0.0 collective-permute-start.1
  71.5 1.5 %collective-permute-done.1 = bf16[8,64,256]{2,1,0:T(8,128)(2,1)S(1)} collective-permute-done((bf16[8,64,256]{2,1,0:T(8,128)(2,1)S(1)}, bf16[8,64,256]{2,1,0:T(8,128)(2,1)S(1)}, u32[]{:S(2)}, u32[]{:S(2)}) %collective-permute-start.1) | collective-permute-done | bytes 262176 | tf_op jit(solution)/shard_map/ppermute | solution.py:257
  73.1 0.1 pad_maximum_fusion
  73.2 1.1 %convolution_convert_fusion = bf16[64,256]{1,0:T(8,128)(2,1)} fusion(bf16[64,4096]{1,0:T(8,128)(2,1)S(1)} %bitcast.24, bf16[4096,256]{1,0:T(8,128)(2,1)S(1)} %copy-done), kind=kOutput, calls=%fused_computation | convolution fusion | flops 134234112 | bytes 2654208 | tf_op jit(solution)/shard_map/dot_general | solution.py:303
  (12 shorter events, 0.3 us)
Async XLA Ops:
  0.6 72.6 %copy-start = (bf16[4096,256]{1,0:T(8,128)(2,1)S(1)}, bf16[4096,256]{1,0:T(8,128)(2,1)}, u32[]{:S(2)}) copy-start(bf16[4096,256]{1,0:T(8,128)(2,1)} %param.21) | copy-start | bytes 6291460
  0.6 10.5 %copy-start.1 = (f32[1024]{0:T(1024)S(1)}, f32[1024]{0:T(1024)}, u32[]{:S(2)}) copy-start(f32[1024]{0:T(1024)} %param.14) | copy-start | bytes 12292
  3.9 20.2 %all-to-all-start = ((bf16[8,4,1024]{2,1,0:T(4,128)(2,1)}), bf16[8,4,1024]{2,1,0:T(4,128)(2,1)S(1)}, u32[]{:S(2)}, u32[]{:S(2)}) async-start(bf16[8,4,1024]{2,1,0:T(4,128)(2,1)} %ask.1), calls=%async_computation | async-start | bytes 131072 | tf_op jit(solution)/shard_map/all_to_all | solution.py:253
  24.1 1.3 %collective-permute-start = (bf16[8,4,1024]{2,1,0:T(4,128)(2,1)S(1)}, bf16[8,4,1024]{2,1,0:T(4,128)(2,1)S(1)}, u32[]{:S(2)}, u32[]{:S(2)}) collective-permute-start(bf16[8,4,1024]{2,1,0:T(4,128)(2,1)S(1)} %all-to-all-done), channel_id=1, source_target_pairs={{0,1},{1,0},{2,3},{3,2},{4,5},{5,4},{6,7},{7,6},{8,9},{9,8},{10,11... | collective-permute-start | bytes 196616 | tf_op jit(solution)/shard_map/ppermute | solution.py:257
  25.7 20.8 %copy-start.3 = (bf16[4,1024]{1,0:T(4,128)(2,1)S(1)}, bf16[4,1024]{1,0:T(4,128)(2,1)}, u32[]{:S(2)}) copy-start(bf16[4,1024]{1,0:T(4,128)(2,1)} %lat_ref.1) | copy-start | bytes 24580
  31.9 16.9 %copy-start.4 = (f32[1024]{0:T(1024)S(1)}, f32[1024]{0:T(1024)}, u32[]{:S(2)}) copy-start(f32[1024]{0:T(1024)} %param.15) | copy-start | bytes 12292
  31.9 28.1 %copy-start.2 = (bf16[1024,256]{1,0:T(8,128)(2,1)S(1)}, bf16[1024,256]{1,0:T(8,128)(2,1)}, u32[]{:S(2)}) copy-start(bf16[1024,256]{1,0:T(8,128)(2,1)} %param.20) | copy-start | bytes 1572868
  71.5 1.5 %collective-permute-start.1 = (bf16[8,64,256]{2,1,0:T(8,128)(2,1)S(1)}, bf16[8,64,256]{2,1,0:T(8,128)(2,1)S(1)}, u32[]{:S(2)}, u32[]{:S(2)}) collective-permute-start(bf16[8,64,256]{2,1,0:T(8,128)(2,1)S(1)} %all_to_all.22), channel_id=1, source_target_pairs={{0,1},{1,0},{2,3},{3,2},{4,5},{5,4},{6,7},{7,6},{8,9},{9,8},{10,11... | collective-permute-start | bytes 786440 | tf_op jit(solution)/shard_map/ppermute | solution.py:257

commit v5 on v0

v5 whole, which is shorter than its diff:
```python
import math

import jax
import jax.numpy as jnp
from jax import lax
from jax.experimental import pallas as pl
from jax.experimental.pallas import tpu as pltpu
from jax.sharding import PartitionSpec as P

HEADS = 16
PACK = 4
LANES = 128
BLOCK = 512
MIB = 1024 * 1024


def norm_rows(values_in, gain):
    center = values_in - jnp.mean(values_in, axis=-1, keepdims=True)
    spread = jnp.mean(center * center, axis=-1, keepdims=True)
    return center * lax.rsqrt(spread + 1e-05) * gain


def in_hbm(array):
    return pltpu.with_memory_space_constraint(array, pltpu.HBM)


def project_rows(get, gain_ref, wk, wv, ks, vs, pns, waits, base, keys_ready=None):
    blocks = len(waits)
    block = pns.shape[1]

    def normed(i):
        return norm_rows(get(i).astype(jnp.float32), gain_ref[...]).astype(jnp.bfloat16)

    def times(weight, i):
        return jnp.dot(pns[i % 2], weight[...], preferred_element_type=jnp.float32).astype(
            jnp.bfloat16
        )

    waits[0][0].wait()
    pns[0] = normed(0)
    for i in range(blocks):
        rows = pl.ds(base + i * block, block)
        if i == 0:
            waits[0][1].wait()
        ks[rows, :] = times(wk, i)
        if keys_ready is not None:
            keys_ready()
        if i == 0:
            waits[0][2].wait()
        if i + 1 < blocks:
            waits[i + 1][0].wait()
            pns[(i + 1) % 2] = normed(i + 1)
        vs[rows, :] = times(wv, i)


def early_kernel(
    x_hbm, gain_hbm, wk_hbm, wv_hbm, k_hbm, v_hbm, gain_ref, xs, wk, wv, ks, vs, pns, sem
):
    gain_copy = pltpu.make_async_copy(gain_hbm, gain_ref, sem.at[3])
    fetches = [
        pltpu.make_async_copy(x_hbm.at[pl.ds(0, xs.shape[0])], xs, sem.at[0]),
        pltpu.make_async_copy(wk_hbm, wk, sem.at[1]),
        pltpu.make_async_copy(wv_hbm, wv, sem.at[2]),
    ]
    gain_copy.start()
    for fetch in fetches:
        fetch.start()
    key_put = pltpu.make_async_copy(ks, k_hbm, sem.at[4])
    value_put = pltpu.make_async_copy(vs, v_hbm, sem.at[5])
    gain_copy.wait()
    project_rows(
        lambda i: xs[...], gain_ref, wk, wv, ks, vs, pns, [fetches], 0, key_put.start
    )
    value_put.start()
    key_put.wait()
    value_put.wait()


def early(patches, gain, w_key, w_value, block):
    width = patches.shape[1]
    hbm = pl.BlockSpec(memory_space=pltpu.HBM)
    return pl.pallas_call(
        early_kernel,
        in_specs=[hbm] * 4,
        out_specs=[hbm] * 2,
        out_shape=[pltpu.HBM((block, width), jnp.bfloat16)] * 2,
        scratch_shapes=[
            pltpu.VMEM((1, width), jnp.float32),
            pltpu.VMEM((block, width), jnp.bfloat16),
            pltpu.VMEM((width, width), jnp.bfloat16),
            pltpu.VMEM((width, width), jnp.bfloat16),
            pltpu.VMEM((block, width), jnp.bfloat16),
            pltpu.VMEM((block, width), jnp.bfloat16),
            pltpu.VMEM((1, block, width), jnp.bfloat16),
            pltpu.SemaphoreType.DMA((6,)),
        ],
        compiler_params=pltpu.CompilerParams(vmem_limit_bytes=24 * MIB),
        cost_estimate=pl.CostEstimate(
            flops=4 * block * width * width,
            transcendentals=block,
            bytes_accessed=6 * block * width + 4 * width * width,
        ),
        name="early",
    )(in_hbm(patches), in_hbm(gain.reshape(1, width)), in_hbm(w_key), in_hbm(w_value))


def attend_kernel(
    lat_ref,
    lat_gain_ref,
    wq_hbm,
    x_hbm,
    gain_hbm,
    wk_hbm,
    wv_hbm,
    k_hbm,
    v_hbm,
    out_ref,
    gain_ref,
    xs,
    wk,
    wv,
    wq,
    ks,
    vs,
    pns,
    x_sem,
    w_sem,
):
    latents, width = lat_ref.shape
    blocks, block, _ = xs.shape
    rows = ks.shape[0]
    head_dim = width // HEADS
    span = PACK * head_dim
    groups = HEADS // PACK
    fetches = [
        pltpu.make_async_copy(x_hbm.at[pl.ds((i + 1) * block, block)], xs.at[i], x_sem.at[i])
        for i in range(blocks)
    ]
    key_copy = pltpu.make_async_copy(wk_hbm, wk, w_sem.at[0])
    value_copy = pltpu.make_async_copy(wv_hbm, wv, w_sem.at[1])
    later = [
        pltpu.make_async_copy(wq_hbm, wq, w_sem.at[2]),
        pltpu.make_async_copy(k_hbm, ks.at[pl.ds(0, block)], w_sem.at[3]),
        pltpu.make_async_copy(v_hbm, vs.at[pl.ds(0, block)], w_sem.at[4]),
    ]
    gain_copy = pltpu.make_async_copy(gain_hbm, gain_ref, w_sem.at[5])
    gain_copy.start()
    fetches[0].start()
    key_copy.start()
    value_copy.start()
    for fetch in fetches[1:] + later:
        fetch.start()
    lat_norm = norm_rows(lat_ref[...].astype(jnp.float32), lat_gain_ref[...]).astype(jnp.bfloat16)
    gain_copy.wait()
    waits = [(fetches[0], key_copy, value_copy)] + [(fetch,) for fetch in fetches[1:]]
    project_rows(lambda i: xs[i], gain_ref, wk, wv, ks, vs, pns, waits, block)
    for fetch in later:
        fetch.wait()
    query = jnp.dot(lat_norm, wq[...], preferred_element_type=jnp.float32).astype(jnp.bfloat16)

    lane_head = lax.broadcasted_iota(jnp.int32, (latents, span), 1) // head_dim
    lane = lax.broadcasted_iota(jnp.int32, (latents, LANES), 1)
    factor = math.log2(math.e) / math.sqrt(head_dim)
    piece = rows if PACK * latents <= 512 else block
    out = jnp.zeros((latents, LANES), jnp.float32)
    for g in range(groups):
        cols = slice(g * span, (g + 1) * span)
        part = query[:, cols]
        apart = jnp.concatenate(
            [jnp.where(lane_head == h, part, jnp.zeros_like(part)) for h in range(PACK)], axis=0
        )
        total = numer = None
        for start in range(0, rows, piece):
            scores = lax.dot_general(
                apart,
                ks[start : start + piece, cols],
                (((1,), (1,)), ((), ())),
                preferred_element_type=jnp.float32,
            )
            expo = jnp.exp2(scores * factor)
            for j in range(piece // LANES):
                lanes = expo[:, j * LANES : (j + 1) * LANES]
                total = lanes if total is None else total + lanes
            here = jnp.dot(
                expo.astype(jnp.bfloat16),
                vs[start : start + piece, cols],
                preferred_element_type=jnp.float32,
            )
            numer = here if numer is None else numer + here
        sums = jnp.sum(total, axis=-1, keepdims=True)
        high = sums.astype(jnp.bfloat16).astype(jnp.float32)
        low = sums - high
        picked = jnp.zeros((latents, span), jnp.float32)
        for h in range(PACK):
            mine = slice(h * latents, (h + 1) * latents)
            picked = jnp.where(lane_head == h, numer[mine], picked)
            out = jnp.where(lane == g * PACK + h, high[mine], out)
            out = jnp.where(lane == HEADS + g * PACK + h, low[mine], out)
        out_ref[:, cols] = picked.astype(jnp.bfloat16)
    out_ref[:, width:] = out.astype(jnp.bfloat16)


def attend(latents, lat_gain, w_query, patches, gain, w_key, w_value, keys, values):
    rows, width = patches.shape
    block = keys.shape[0]
    blocks = rows // block - 1
    count = latents.shape[0]
    vmem = pl.BlockSpec(memory_space=pltpu.VMEM)
    hbm = pl.BlockSpec(memory_space=pltpu.HBM)
    return pl.pallas_call(
        attend_kernel,
        in_specs=[vmem, vmem] + [hbm] * 7,
        out_specs=vmem,
        out_shape=jax.ShapeDtypeStruct((count, width + LANES), jnp.bfloat16),
        scratch_shapes=[
            pltpu.VMEM((1, width), jnp.float32),
            pltpu.VMEM((blocks, block, width), jnp.bfloat16),
            pltpu.VMEM((width, width), jnp.bfloat16),
            pltpu.VMEM((width, width), jnp.bfloat16),
            pltpu.VMEM((width, width), jnp.bfloat16),
            pltpu.VMEM((rows, width), jnp.bfloat16),
            pltpu.VMEM((rows, width), jnp.bfloat16),
            pltpu.VMEM((2, block, width), jnp.bfloat16),
            pltpu.SemaphoreType.DMA((blocks,)),
            pltpu.SemaphoreType.DMA((6,)),
        ],
        compiler_params=pltpu.CompilerParams(vmem_limit_bytes=42 * MIB),
        cost_estimate=pl.CostEstimate(
            flops=4 * (rows - block) * width * width + 4 * rows * count * PACK * width,
            transcendentals=rows * count * HEADS,
            bytes_accessed=2 * rows * width + 6 * width * width,
        ),
        name="attend",
    )(
        latents,
        lat_gain.reshape(1, width),
        in_hbm(w_query),
        in_hbm(patches),
        in_hbm(gain.reshape(1, width)),
        in_hbm(w_key),
        in_hbm(w_value),
        in_hbm(keys),
        in_hbm(values),
    )


def exchange(blocks):
    return lax.all_to_all(blocks, "page", 0, 0, tiled=True)


def spread(block, count):
    return jnp.broadcast_to(block[None], (count,) + block.shape)


def exchange_side(blocks, count):
    sides = [[2 * chip + side for chip in range(count // 2)] for side in range(2)]
    return lax.all_to_all(blocks, "page", 0, 0, axis_index_groups=sides, tiled=True)


def join_sides(mine, count):
    theirs = lax.ppermute(mine, "page", [(i, i ^ 1) for i in range(count)])
    even = lax.axis_index("page") % 2 == 0
    both = jnp.stack([jnp.where(even, mine, theirs), jnp.where(even, theirs, mine)], axis=1)
    return both.reshape((count,) + mine.shape[1:])


def body(
    latents,
    patches,
    lat_gain,
    patch_gain,
    mlp_gain,
    w_query,
    w_key,
    w_value,
    w_out,
    w_hidden,
    w_connect,
):
    count = lax.axis_size("page")
    lat_rows, width = latents.shape
    lat_all = exchange(spread(latents, count)).reshape(count * lat_rows, width)
    block = math.gcd(patches.shape[0], BLOCK)
    keys, values = early(patches, patch_gain, w_key, w_value, block)
    packed = attend(
        lat_all, lat_gain, w_query, patches, patch_gain, w_key, w_value, keys, values
    )
    parts = exchange(packed.reshape(count, lat_rows, width + LANES))
    summed = jnp.sum(parts.astype(jnp.float32), axis=0)
    denom = summed[:, width : width + HEADS] + summed[:, width + HEADS : width + 2 * HEADS]
    attended = (
        (summed[:, :width].reshape(lat_rows, HEADS, width // HEADS) / denom[:, :, None])
        .reshape(lat_rows, width)
        .astype(jnp.bfloat16)
    )
    mixed = latents.astype(jnp.float32) + jnp.dot(
        attended, w_out, preferred_element_type=jnp.float32
    )
    resampled = mixed.astype(jnp.bfloat16)
    mlp_in = norm_rows(mixed, mlp_gain).astype(jnp.bfloat16)
    mlp_all = exchange(spread(mlp_in, count)).reshape(count * lat_rows, width)
    hidden = jax.nn.gelu(
        jnp.dot(mlp_all, w_hidden, preferred_element_type=jnp.float32), approximate=True
    ).astype(jnp.bfloat16)
    rows, units = hidden.shape
    hidden_all = join_sides(exchange_side(spread(hidden, count // 2), count), count)
    hidden_all = jnp.transpose(hidden_all, (1, 0, 2)).reshape(rows, count * units)
    connector = jnp.dot(hidden_all, w_connect, preferred_element_type=jnp.float32).astype(
        jnp.bfloat16
    )
    return (resampled, connector)


def solution(mesh):
    placed = (
        P(("slab", "page"), None),
        P(("slab", "page"), None),
        P(),
        P(),
        P(),
        P(),
        P(),
        P(),
        P(),
        P(None, "page"),
        P(None, "page"),
    )
    return jax.shard_map(
        body,
        mesh=mesh,
        in_specs=placed,
        out_specs=(P(("slab", "page"), None), P("slab", "page")),
        check_vma=False,
    )
```

time: 256 us -> 70.4 us (0.28)
  blocking collectives: 94 us -> 33.5 us
  waiting for transfers between devices: 55.7 us -> 3.94 us
  matrix products: 45.5 us -> 3.4 us
  local copies, waits for them, and re-layouts: 32.6 us -> 1.92 us
  Pallas kernels: 0 us -> 18 us
  between operations: 14.9 us -> 0.79 us
  starting transfers between devices: 0.04 us -> 7.39 us
  other arithmetic: 6.74 us -> 1.06 us
  loops' own time: 5.42 us -> 0 us
    all_gather x3 -> x0, blocking collectives: 63.5 us -> none  [the longest x1 23.4 us: body(): query_all = lax.all_gather(query, 'page', axis=0, tiled=True)]
    unnamed x2 -> x0, waiting for transfers between devices: 55.7 us -> none
    dot_general x21 -> x2, matrix products: 43.4 us -> 1.31 us  [the longest x1 1.08 us: body(): jnp.dot(hidden_all, w_connect, preferred_element_type=jnp.float32)]
    all_to_all x0 -> x3, blocking collectives: none -> 33.5 us  [the longest x2 22.3 us: exchange(): return lax.all_to_all(blocks, 'page', 0, 0, tiled=True)]
    unnamed x1 -> x0, blocking collectives: 30.5 us -> none
    dynamic_slice x40 -> x0, local copies, waits for them, and re-layouts: 25.4 us -> none  [the longest x16 19 us: head_pair(): lax.dynamic_slice_in_dim(keys, column, group_width, 1)]
    pallas_call x0 -> x2, Pallas kernels: none -> 18 us  [the longest x1 12.5 us: attend(): pl.pallas_call(attend_kernel, in_specs=[vmem, vmem] + [hbm] * 7, out_spec...]
    all_to_all x0 -> x1, starting transfers between devices: none -> 7.39 us  [exchange(): return lax.all_to_all(blocks, 'page', 0, 0, tiled=True)]
  transfers between devices with their start and end apart: 1 -> 2, of which waited for: 1 -> 2; matrix products, arithmetic and copies ran while one was open for 0% -> 0% of each run, Pallas kernels for 0% -> 8%
where the time goes in v5:
time: 70.4 us; the launch traced here: 70 us
  blocking collectives  33.5 us (48%)
  Pallas kernels  18 us (26%)
  starting transfers between devices  7.39 us (10%)
  waiting for transfers between devices  3.94 us (6%)
  matrix products  3.4 us (5%)
  local copies, waits for them, and re-layouts  1.92 us (3%)
  other arithmetic  1.06 us (2%)
  between operations  0.79 us (1%)
    all_to_all x2, blocking collectives, exchange(): return lax.all_to_all(blocks, 'page', 0, 0, tiled=True)  22.3 us
    pallas_call x1, Pallas kernels, attend(): pl.pallas_call(attend_kernel, in_specs=[vmem, vmem] + [hbm] * 7, out_spec...  12.5 us
    all_to_all x1, blocking collectives, exchange_side(): lax.all_to_all(blocks, 'page', 0, 0, axis_index_groups=sides, tiled=True)  11.2 us
    all_to_all x1, starting transfers between devices, exchange(): return lax.all_to_all(blocks, 'page', 0, 0, tiled=True)  7.39 us
    pallas_call x1, Pallas kernels, early(): pl.pallas_call(early_kernel, in_specs=[hbm] * 4, out_specs=[hbm] * 2, out...  5.51 us
    all_to_all x1, waiting for transfers between devices, exchange(): return lax.all_to_all(blocks, 'page', 0, 0, tiled=True)  2.41 us
    dot_general x1, matrix products, body(): jnp.dot(attended, w_out, preferred_element_type=jnp.float32)  2.09 us
    broadcast_in_dim x3, local copies, waits for them, and re-layouts, spread(): return jnp.broadcast_to(block[None], (count,) + block.shape)  1.59 us
  transfers between devices with their start and end apart: 2, of which 2 were waited for; matrix products, arithmetic and copies ran while one was open for 0% of the time, Pallas kernels for 8%

profile of v5, /device:TPU:0, one launch (start us, length us, event | category | flops | bytes accessed | tf_op | source)
XLA Modules:
  0.0 70.0 jit_solution(451269469499284568)
XLA Ops:
  0.6 0.0 copy-start
  0.6 1.5 %broadcast_in_dim.6 = bf16[16,4,1024]{2,1,0:T(4,128)(2,1)} broadcast(bf16[4,1024]{1,0:T(4,128)(2,1)} %param.11), dimensions={1,2} | broadcast | bytes 139264 | tf_op jit(solution)/shard_map/broadcast_in_dim | solution.py:252
  2.2 7.4 %all-to-all-start = ((bf16[16,4,1024]{2,1,0:T(4,128)(2,1)}), bf16[16,4,1024]{2,1,0:T(4,128)(2,1)S(1)}, u32[]{:S(2)}, u32[]{:S(2)}) async-start(bf16[16,4,1024]{2,1,0:T(4,128)(2,1)} %broadcast_in_dim.6), calls=%async_computation | async-start | bytes 262144 | tf_op jit(solution)/shard_map/all_to_all | solution.py:248
  9.6 0.0 copy-start.1
  9.6 5.5 %early.1 = (bf16[512,1024]{1,0:T(8,128)(2,1)}, bf16[512,1024]{1,0:T(8,128)(2,1)}) custom-call(bf16[2048,1024]{1,0:T(8,128)(2,1)} %x_hbm.3, f32[1,1024]{1,0:T(1,128)} %bitcast.21, bf16[1024,1024]{1,0:T(8,128)(2,1)} %wk_hbm.3, bf16[1024,1024]{1,0:T(8,128)(2,1)} %wv_hbm.3), custom_call_target="tpu_custom_call" | custom-call | flops 2147483648 | bytes 7340032 | tf_op jit(solution)/shard_map/early/pallas_call | solution.py:82
  15.1 2.4 %all-to-all-done = bf16[16,4,1024]{2,1,0:T(4,128)(2,1)S(1)} async-done(((bf16[16,4,1024]{2,1,0:T(4,128)(2,1)}), bf16[16,4,1024]{2,1,0:T(4,128)(2,1)S(1)}, u32[]{:S(2)}, u32[]{:S(2)}) %all-to-all-start) | async-done | bytes 131104 | tf_op jit(solution)/shard_map/all_to_all | solution.py:248
  17.5 0.0 copy-done.1
  17.6 0.0 copy-start.3
  17.6 12.5 %attend.1 = bf16[64,1152]{1,0:T(8,128)(2,1)S(1)} custom-call(bf16[64,1024]{1,0:T(8,128)(2,1)S(1)} %reshape.46.lat_ref, f32[1,1024]{1,0:T(1,128)S(1)} %bitcast.18, bf16[1024,1024]{1,0:T(8,128)(2,1)} %wq_hbm.1, bf16[2048,1024]{1,0:T(8,128)(2,1)} %x_hbm.3, f32[1,1024]{1,0:T(1,128)} %bitcast.22, bf16[1024,1024]{1,0:T(8,128)(2,1)} %wk_hbm.3, ...), custom_call_target="tpu_custom_call" | custom-call | flops 8589934592 | bytes 10485760 | tf_op jit(solution)/shard_map/attend/pallas_call | solution.py:210
  30.1 0.0 copy-start.4
  30.1 0.0 copy-start.2
  30.1 11.7 %all_to_all.20 = bf16[16,4,1152]{2,1,0:T(4,128)(2,1)S(1)} all-to-all(bf16[16,4,1152]{2,1,0:T(4,128)(2,1)S(1)} %reshape.49), channel_id=1, replica_groups=mesh['slab'=2,'page'=16] {'page'}, dimensions={0} | all-to-all | bytes 294912 | tf_op jit(solution)/shard_map/all_to_all | solution.py:248
  41.9 0.1 convert_reduce_fusion
  41.9 0.1 slice_add_fusion
  42.0 0.1 div.17
  42.1 0.1 div.18
  42.2 0.0 copy-done.3
  42.2 2.1 %fusion.10 = (f32[4]{0:T(128)S(1)}, f32[4,1024]{1,0:T(4,128)S(1)}) fusion(bf16[1024,1024]{1,0:T(8,128)(2,1)} %param.19, f32[4,1024]{1,0:T(4,128)S(1)} %div.18, f32[4,1152]{1,0:T(4,128)S(1)} %convert_reduce_fusion, bf16[4,1024]{1,0:T(4,128)(2,1)S(1)} %copy-done.3), kind=kOutput, calls=%fused_computation.22 | convolution fusion | flops 8409084 | bytes 2154512 | tf_op jit(solution)/shard_map/dot_general | solution.py:296
  44.3 0.2 multiply_reduce_fusion
  44.5 0.0 copy-done.4
  44.5 0.6 multiply_convert_fusion
  45.2 10.5 %all_to_all.21 = bf16[16,4,1024]{2,1,0:T(4,128)(2,1)S(1)} all-to-all(bf16[16,4,1024]{2,1,0:T(4,128)(2,1)S(1)} %broadcast_in_dim.7), channel_id=1, replica_groups=mesh['slab'=2,'page'=16] {'page'}, dimensions={0} | all-to-all | bytes 262144 | tf_op jit(solution)/shard_map/all_to_all | solution.py:248
  55.7 0.0 copy-done.2
  55.7 0.2 fusion.7
  56.0 11.2 %all_to_all.22 = bf16[8,64,256]{2,1,0:T(8,128)(2,1)S(1)} all-to-all(bf16[8,64,256]{2,1,0:T(8,128)(2,1)S(1)} %broadcast_in_dim.8), channel_id=1, replica_groups={{0,2,4,6,8,10,12,14},{1,3,5,7,9,11,13,15},{16,18,20,22,24,26,28,30},{17..., dimensions={0} | all-to-all | bytes 524288 | tf_op jit(solution)/shard_map/all_to_all | solution.py:257
  67.2 0.0 collective-permute-start
  67.2 1.5 %collective-permute-done = bf16[8,64,256]{2,1,0:T(8,128)(2,1)S(1)} collective-permute-done((bf16[8,64,256]{2,1,0:T(8,128)(2,1)S(1)}, bf16[8,64,256]{2,1,0:T(8,128)(2,1)S(1)}, u32[]{:S(2)}, u32[]{:S(2)}) %collective-permute-start) | collective-permute-done | bytes 262176 | tf_op jit(solution)/shard_map/ppermute | solution.py:261
  68.8 0.1 pad_maximum_fusion
  68.9 0.0 copy-done
  68.9 1.1 %convolution_convert_fusion = bf16[64,256]{1,0:T(8,128)(2,1)} fusion(bf16[64,4096]{1,0:T(8,128)(2,1)S(1)} %bitcast.20, bf16[4096,256]{1,0:T(8,128)(2,1)S(1)} %copy-done), kind=kOutput, calls=%fused_computation | convolution fusion | flops 134234112 | bytes 2654208 | tf_op jit(solution)/shard_map/dot_general | solution.py:308
  (9 shorter events, 0.3 us)
Async XLA Ops:
  0.6 68.3 %copy-start = (bf16[4096,256]{1,0:T(8,128)(2,1)S(1)}, bf16[4096,256]{1,0:T(8,128)(2,1)}, u32[]{:S(2)}) copy-start(bf16[4096,256]{1,0:T(8,128)(2,1)} %param.21) | copy-start | bytes 6291460
  2.2 15.3 %all-to-all-start = ((bf16[16,4,1024]{2,1,0:T(4,128)(2,1)}), bf16[16,4,1024]{2,1,0:T(4,128)(2,1)S(1)}, u32[]{:S(2)}, u32[]{:S(2)}) async-start(bf16[16,4,1024]{2,1,0:T(4,128)(2,1)} %broadcast_in_dim.6), calls=%async_computation | async-start | bytes 262144 | tf_op jit(solution)/shard_map/all_to_all | solution.py:248
  9.6 8.0 %copy-start.1 = (f32[1024]{0:T(1024)S(1)}, f32[1024]{0:T(1024)}, u32[]{:S(2)}) copy-start(f32[1024]{0:T(1024)} %param.13) | copy-start | bytes 12292
  17.6 24.6 %copy-start.3 = (bf16[4,1024]{1,0:T(4,128)(2,1)S(1)}, bf16[4,1024]{1,0:T(4,128)(2,1)}, u32[]{:S(2)}) copy-start(bf16[4,1024]{1,0:T(4,128)(2,1)} %param.11) | copy-start | bytes 24580
  30.1 14.4 %copy-start.4 = (f32[1024]{0:T(1024)S(1)}, f32[1024]{0:T(1024)}, u32[]{:S(2)}) copy-start(f32[1024]{0:T(1024)} %param.15) | copy-start | bytes 12292
  30.1 25.6 %copy-start.2 = (bf16[1024,256]{1,0:T(8,128)(2,1)S(1)}, bf16[1024,256]{1,0:T(8,128)(2,1)}, u32[]{:S(2)}) copy-start(bf16[1024,256]{1,0:T(8,128)(2,1)} %param.20) | copy-start | bytes 1572868
  67.2 1.5 %collective-permute-start = (bf16[8,64,256]{2,1,0:T(8,128)(2,1)S(1)}, bf16[8,64,256]{2,1,0:T(8,128)(2,1)S(1)}, u32[]{:S(2)}, u32[]{:S(2)}) collective-permute-start(bf16[8,64,256]{2,1,0:T(8,128)(2,1)S(1)} %all_to_all.22), channel_id=1, source_target_pairs={{0,1},{1,0},{2,3},{3,2},{4,5},{5,4},{6,7},{7,6},{8,9},{9,8},{10,11... | collective-permute-start | bytes 786440 | tf_op jit(solution)/shard_map/ppermute | solution.py:261

commit v6 on v5

--- a/solution.py
+++ b/solution.py
@@ -11,6 +11,7 @@
 PACK = 4
 LANES = 128
 BLOCK = 512
+CHUNKS = 4
 MIB = 1024 * 1024
 
 
@@ -41,8 +42,15 @@
     for i in range(blocks):
         rows = pl.ds(base + i * block, block)
         if i == 0:
-            waits[0][1].wait()
-        ks[rows, :] = times(wk, i)
+            size = ks.shape[1] // len(waits[0][1])
+            for j, fetch in enumerate(waits[0][1]):
+                cols = pl.ds(j * size, size)
+                fetch.wait()
+                ks[rows, cols] = jnp.dot(
+                    pns[0], wk[:, cols], preferred_element_type=jnp.float32
+                ).astype(jnp.bfloat16)
+        else:
+            ks[rows, :] = times(wk, i)
         if keys_ready is not None:
             keys_ready()
         if i == 0:
@@ -53,20 +61,29 @@
         vs[rows, :] = times(wv, i)
 
 
+def column_copies(hbm, ref, sem):
+    size = ref.shape[1] // CHUNKS
+    return [
+        pltpu.make_async_copy(
+            hbm.at[:, pl.ds(j * size, size)], ref.at[:, pl.ds(j * size, size)], sem.at[j]
+        )
+        for j in range(CHUNKS)
+    ]
+
+
 def early_kernel(
-    x_hbm, gain_hbm, wk_hbm, wv_hbm, k_hbm, v_hbm, gain_ref, xs, wk, wv, ks, vs, pns, sem
+    x_hbm, gain_hbm, wk_hbm, wv_hbm, k_hbm, v_hbm, gain_ref, xs, wk, wv, ks, vs, pns, sem, wk_sem
 ):
-    gain_copy = pltpu.make_async_copy(gain_hbm, gain_ref, sem.at[3])
-    fetches = [
-        pltpu.make_async_copy(x_hbm.at[pl.ds(0, xs.shape[0])], xs, sem.at[0]),
-        pltpu.make_async_copy(wk_hbm, wk, sem.at[1]),
-        pltpu.make_async_copy(wv_hbm, wv, sem.at[2]),
-    ]
+    gain_copy = pltpu.make_async_copy(gain_hbm, gain_ref, sem.at[2])
+    x_copy = pltpu.make_async_copy(x_hbm.at[pl.ds(0, xs.shape[0])], xs, sem.at[0])
+    key_copies = column_copies(wk_hbm, wk, wk_sem)
+    value_copy = pltpu.make_async_copy(wv_hbm, wv, sem.at[1])
+    fetches = (x_copy, key_copies, value_copy)
     gain_copy.start()
-    for fetch in fetches:
+    for fetch in [x_copy] + key_copies + [value_copy]:
         fetch.start()
-    key_put = pltpu.make_async_copy(ks, k_hbm, sem.at[4])
-    value_put = pltpu.make_async_copy(vs, v_hbm, sem.at[5])
+    key_put = pltpu.make_async_copy(ks, k_hbm, sem.at[3])
+    value_put = pltpu.make_async_copy(vs, v_hbm, sem.at[4])
     gain_copy.wait()
     project_rows(
         lambda i: xs[...], gain_ref, wk, wv, ks, vs, pns, [fetches], 0, key_put.start
@@ -92,7 +109,8 @@
             pltpu.VMEM((block, width), jnp.bfloat16),
             pltpu.VMEM((block, width), jnp.bfloat16),
             pltpu.VMEM((1, block, width), jnp.bfloat16),
-            pltpu.SemaphoreType.DMA((6,)),
+            pltpu.SemaphoreType.DMA((5,)),
+            pltpu.SemaphoreType.DMA((CHUNKS,)),
         ],
         compiler_params=pltpu.CompilerParams(vmem_limit_bytes=24 * MIB),
         cost_estimate=pl.CostEstimate(
@@ -125,6 +143,7 @@
     pns,
     x_sem,
     w_sem,
+    wk_sem,
 ):
     latents, width = lat_ref.shape
     blocks, block, _ = xs.shape
@@ -136,23 +155,24 @@
         pltpu.make_async_copy(x_hbm.at[pl.ds((i + 1) * block, block)], xs.at[i], x_sem.at[i])
         for i in range(blocks)
     ]
-    key_copy = pltpu.make_async_copy(wk_hbm, wk, w_sem.at[0])
-    value_copy = pltpu.make_async_copy(wv_hbm, wv, w_sem.at[1])
+    key_copies = column_copies(wk_hbm, wk, wk_sem)
+    value_copy = pltpu.make_async_copy(wv_hbm, wv, w_sem.at[0])
     later = [
-        pltpu.make_async_copy(wq_hbm, wq, w_sem.at[2]),
-        pltpu.make_async_copy(k_hbm, ks.at[pl.ds(0, block)], w_sem.at[3]),
-        pltpu.make_async_copy(v_hbm, vs.at[pl.ds(0, block)], w_sem.at[4]),
-    ]
-    gain_copy = pltpu.make_async_copy(gain_hbm, gain_ref, w_sem.at[5])
+        pltpu.make_async_copy(wq_hbm, wq, w_sem.at[1]),
+        pltpu.make_async_copy(k_hbm, ks.at[pl.ds(0, block)], w_sem.at[2]),
+        pltpu.make_async_copy(v_hbm, vs.at[pl.ds(0, block)], w_sem.at[3]),
+    ]
+    gain_copy = pltpu.make_async_copy(gain_hbm, gain_ref, w_sem.at[4])
     gain_copy.start()
     fetches[0].start()
-    key_copy.start()
+    for fetch in key_copies:
+        fetch.start()
     value_copy.start()
     for fetch in fetches[1:] + later:
         fetch.start()
     lat_norm = norm_rows(lat_ref[...].astype(jnp.float32), lat_gain_ref[...]).astype(jnp.bfloat16)
     gain_copy.wait()
-    waits = [(fetches[0], key_copy, value_copy)] + [(fetch,) for fetch in fetches[1:]]
+    waits = [(fetches[0], key_copies, value_copy)] + [(fetch,) for fetch in fetches[1:]]
     project_rows(lambda i: xs[i], gain_ref, wk, wv, ks, vs, pns, waits, block)
     for fetch in later:
         fetch.wait()
@@ -222,7 +242,8 @@
             pltpu.VMEM((rows, width), jnp.bfloat16),
             pltpu.VMEM((2, block, width), jnp.bfloat16),
             pltpu.SemaphoreType.DMA((blocks,)),
-            pltpu.SemaphoreType.DMA((6,)),
+            pltpu.SemaphoreType.DMA((5,)),
+            pltpu.SemaphoreType.DMA((CHUNKS,)),
         ],
         compiler_params=pltpu.CompilerParams(vmem_limit_bytes=42 * MIB),
         cost_estimate=pl.CostEstimate(
@@ -244,6 +265,29 @@
     )
 
 
+def copies_kernel(x_hbm, out_hbm, sem):
+    puts = [
+        pltpu.make_async_copy(x_hbm, out_hbm.at[j], sem.at[j]) for j in range(out_hbm.shape[0])
+    ]
+    for put in puts:
+        put.start()
+    for put in puts:
+        put.wait()
+
+
+def copies(block, count):
+    hbm = pl.BlockSpec(memory_space=pltpu.HBM)
+    return pl.pallas_call(
+        copies_kernel,
+        in_specs=[hbm],
+        out_specs=hbm,
+        out_shape=jax.ShapeDtypeStruct((count,) + block.shape, block.dtype),
+        scratch_shapes=[pltpu.SemaphoreType.DMA((count,))],
+        compiler_params=pltpu.CompilerParams(vmem_limit_bytes=MIB),
+        name="copies",
+    )(in_hbm(block))
+
+
 def exchange(blocks):
     return lax.all_to_all(blocks, "page", 0, 0, tiled=True)
 
@@ -257,11 +301,12 @@
     return lax.all_to_all(blocks, "page", 0, 0, axis_index_groups=sides, tiled=True)
 
 
-def join_sides(mine, count):
-    theirs = lax.ppermute(mine, "page", [(i, i ^ 1) for i in range(count)])
-    even = lax.axis_index("page") % 2 == 0
-    both = jnp.stack([jnp.where(even, mine, theirs), jnp.where(even, theirs, mine)], axis=1)
-    return both.reshape((count,) + mine.shape[1:])
+def swap_cores(array, count):
+    return lax.ppermute(array, "page", [(i, i ^ 1) for i in range(count)])
+
+
+def by_side(even, mine, theirs, axis):
+    return jnp.concatenate([jnp.where(even, mine, theirs), jnp.where(even, theirs, mine)], axis=axis)
 
 
 def body(
@@ -279,9 +324,13 @@
 ):
     count = lax.axis_size("page")
     lat_rows, width = latents.shape
-    lat_all = exchange(spread(latents, count)).reshape(count * lat_rows, width)
+    lat_all = exchange(copies(latents, count)).reshape(count * lat_rows, width)
     block = math.gcd(patches.shape[0], BLOCK)
     keys, values = early(patches, patch_gain, w_key, w_value, block)
+    even = lax.axis_index("page") % 2 == 0
+    lat_all, w_theirs, even = lax.optimization_barrier(
+        (lat_all, swap_cores(w_hidden, count), even)
+    )
     packed = attend(
         lat_all, lat_gain, w_query, patches, patch_gain, w_key, w_value, keys, values
     )
@@ -298,16 +347,28 @@
     )
     resampled = mixed.astype(jnp.bfloat16)
     mlp_in = norm_rows(mixed, mlp_gain).astype(jnp.bfloat16)
-    mlp_all = exchange(spread(mlp_in, count)).reshape(count * lat_rows, width)
-    hidden = jax.nn.gelu(
-        jnp.dot(mlp_all, w_hidden, preferred_element_type=jnp.float32), approximate=True
-    ).astype(jnp.bfloat16)
-    rows, units = hidden.shape
-    hidden_all = join_sides(exchange_side(spread(hidden, count // 2), count), count)
-    hidden_all = jnp.transpose(hidden_all, (1, 0, 2)).reshape(rows, count * units)
-    connector = jnp.dot(hidden_all, w_connect, preferred_element_type=jnp.float32).astype(
-        jnp.bfloat16
-    )
+    chips = count // 2
+    rows = chips * lat_rows
+    mlp_side = exchange_side(spread(mlp_in, chips), count).reshape(rows, width)
+
+    def hidden_of(weight):
+        return jax.nn.gelu(
+            jnp.dot(mlp_side, weight, preferred_element_type=jnp.float32), approximate=True
+        ).astype(jnp.bfloat16)
+
+    hidden = by_side(even, hidden_of(w_hidden), hidden_of(w_theirs), 1)
+    hidden_mine = exchange_side(spread(hidden, chips), count)
+    hidden_theirs = swap_cores(hidden_mine, count)
+
+    def connect(blocks):
+        flat = jnp.transpose(blocks, (1, 0, 2)).reshape(rows, w_connect.shape[0])
+        return jnp.dot(flat, w_connect, preferred_element_type=jnp.float32).astype(jnp.bfloat16)
+
+    sides = [
+        part.reshape(chips, 1, lat_rows, w_connect.shape[1])
+        for part in (connect(hidden_mine), connect(hidden_theirs))
+    ]
+    connector = by_side(even, sides[0], sides[1], 1).reshape(count * lat_rows, w_connect.shape[1])
     return (resampled, connector)
 
 

time: 70.4 us -> 76.5 us (1.087)
  Pallas kernels: 18 us -> 27.1 us
  waiting for transfers between devices: 3.94 us -> 1.59 us
  local copies, waits for them, and re-layouts: 1.92 us -> 1.04 us
    all_to_all x1 -> x2, blocking collectives: 11.2 us -> 19.9 us  [exchange_side(): lax.all_to_all(blocks, 'page', 0, 0, axis_index_groups=sides, tiled=True)]
    all_to_all x2 -> x1, blocking collectives: 22.3 us -> 13.6 us  [exchange(): return lax.all_to_all(blocks, 'page', 0, 0, tiled=True)]
    pallas_call x0 -> x1, Pallas kernels: none -> 5.22 us  [copies(): pl.pallas_call(copies_kernel, in_specs=[hbm], out_specs=hbm, out_shape=ja...]
    pallas_call x1, Pallas kernels: 12.5 us -> 14.5 us  [attend(): pl.pallas_call(attend_kernel, in_specs=[vmem, vmem] + [hbm] * 7, out_spec...]
    all_to_all x1, waiting for transfers between devices: 2.41 us -> 0.54 us  [exchange(): return lax.all_to_all(blocks, 'page', 0, 0, tiled=True)]
    pallas_call x1, Pallas kernels: 5.51 us -> 7.36 us  [early(): pl.pallas_call(early_kernel, in_specs=[hbm] * 4, out_specs=[hbm] * 2, out...]
    broadcast_in_dim x3 -> x2, local copies, waits for them, and re-layouts: 1.59 us -> 0.04 us  [spread(): return jnp.broadcast_to(block[None], (count,) + block.shape)]
    ppermute x1 -> x2, waiting for transfers between devices: 1.53 us -> 1.05 us  [swap_cores(): return lax.ppermute(array, 'page', [(i, i ^ 1) for i in range(count)])]
  transfers between devices with their start and end apart: 2 -> 3, of which waited for: 2 -> 2; matrix products, arithmetic and copies ran while one was open for 0% -> 1% of each run, Pallas kernels for 8% -> 17%
where the time goes in v6:
time: 76.5 us; the launch traced here: 76.1 us
  blocking collectives  33.5 us (44%)
  Pallas kernels  27.1 us (35%)
  starting transfers between devices  7.65 us (10%)
  matrix products  3.43 us (4%)
  waiting for transfers between devices  1.59 us (2%)
  local copies, waits for them, and re-layouts  1.04 us (1%)
  other arithmetic  1 us (1%)
  between operations  0.85 us (1%)
    all_to_all x2, blocking collectives, exchange_side(): lax.all_to_all(blocks, 'page', 0, 0, axis_index_groups=sides, tiled=True)  19.9 us
    pallas_call x1, Pallas kernels, attend(): pl.pallas_call(attend_kernel, in_specs=[vmem, vmem] + [hbm] * 7, out_spec...  14.5 us
    all_to_all x1, blocking collectives, exchange(): return lax.all_to_all(blocks, 'page', 0, 0, tiled=True)  13.6 us
    pallas_call x1, Pallas kernels, early(): pl.pallas_call(early_kernel, in_specs=[hbm] * 4, out_specs=[hbm] * 2, out...  7.36 us
    all_to_all x1, starting transfers between devices, exchange(): return lax.all_to_all(blocks, 'page', 0, 0, tiled=True)  7.06 us
    pallas_call x1, Pallas kernels, copies(): pl.pallas_call(copies_kernel, in_specs=[hbm], out_specs=hbm, out_shape=ja...  5.22 us
    dot_general x1, matrix products, body(): jnp.dot(attended, w_out, preferred_element_type=jnp.float32)  2.09 us
  transfers between devices with their start and end apart: 3, of which 2 were waited for; matrix products, arithmetic and copies ran while one was open for 1% of the time, Pallas kernels for 17%

profile of v6, /device:TPU:0, one launch (start us, length us, event | category | flops | bytes accessed | tf_op | source)
XLA Modules:
  0.0 76.1 jit_solution(11922768732614353615)
XLA Ops:
  0.6 0.0 copy-start
  0.6 0.5 collective-permute-start
  1.2 5.2 %copies.1 = bf16[16,4,1024]{2,1,0:T(4,128)(2,1)} custom-call(bf16[4,1024]{1,0:T(4,128)(2,1)} %x_hbm.3), custom_call_target="tpu_custom_call" | custom-call | tf_op jit(solution)/shard_map/copies/pallas_call | solution.py:280
  6.4 7.1 %all-to-all-start = ((bf16[16,4,1024]{2,1,0:T(4,128)(2,1)}), bf16[16,4,1024]{2,1,0:T(4,128)(2,1)S(1)}, u32[]{:S(2)}, u32[]{:S(2)}) async-start(bf16[16,4,1024]{2,1,0:T(4,128)(2,1)} %copies.1), calls=%async_computation | async-start | bytes 262144 | tf_op jit(solution)/shard_map/all_to_all | solution.py:292
  13.5 0.0 copy-start.1
  13.5 7.4 %early.1 = (bf16[512,1024]{1,0:T(8,128)(2,1)}, bf16[512,1024]{1,0:T(8,128)(2,1)}) custom-call(bf16[2048,1024]{1,0:T(8,128)(2,1)} %x_hbm.5, f32[1,1024]{1,0:T(1,128)} %bitcast.22, bf16[1024,1024]{1,0:T(8,128)(2,1)} %wk_hbm.3, bf16[1024,1024]{1,0:T(8,128)(2,1)} %wv_hbm.3), custom_call_target="tpu_custom_call" | custom-call | flops 2147483648 | bytes 7340032 | tf_op jit(solution)/shard_map/early/pallas_call | solution.py:99
  20.8 0.5 all-to-all-done
  21.4 0.0 collective-permute-done
  21.4 0.0 copy-done.1
  21.4 0.0 copy-start.3
  21.5 14.5 %attend.1 = bf16[64,1152]{1,0:T(8,128)(2,1)S(1)} custom-call(bf16[64,1024]{1,0:T(8,128)(2,1)S(1)} %reshape.94.lat_ref, f32[1,1024]{1,0:T(1,128)S(1)} %bitcast.17, bf16[1024,1024]{1,0:T(8,128)(2,1)} %wq_hbm.1, bf16[2048,1024]{1,0:T(8,128)(2,1)} %x_hbm.5, f32[1,1024]{1,0:T(1,128)} %bitcast.23, bf16[1024,1024]{1,0:T(8,128)(2,1)} %wk_hbm.3, ...), custom_call_target="tpu_custom_call" | custom-call | flops 8589934592 | bytes 10485760 | tf_op jit(solution)/shard_map/attend/pallas_call | solution.py:230
  35.9 0.0 copy-start.4
  36.0 0.0 copy-start.2
  36.0 13.6 %all_to_all.20 = bf16[16,4,1152]{2,1,0:T(4,128)(2,1)S(1)} all-to-all(bf16[16,4,1152]{2,1,0:T(4,128)(2,1)S(1)} %reshape.97), channel_id=1, replica_groups=mesh['slab'=2,'page'=16] {'page'}, dimensions={0} | all-to-all | bytes 294912 | tf_op jit(solution)/shard_map/all_to_all | solution.py:292
  49.6 0.1 convert_reduce_fusion
  49.7 0.1 slice_add_fusion
  49.8 0.1 div.17
  49.8 0.1 div.18
  49.9 0.0 copy-done.3
  49.9 2.1 %fusion.18 = (f32[4]{0:T(128)S(1)}, f32[4,1024]{1,0:T(4,128)S(1)}) fusion(bf16[1024,1024]{1,0:T(8,128)(2,1)} %param.19, f32[4,1024]{1,0:T(4,128)S(1)} %div.18, f32[4,1152]{1,0:T(4,128)S(1)} %convert_reduce_fusion, bf16[4,1024]{1,0:T(4,128)(2,1)S(1)} %copy-done.3), kind=kOutput, calls=%fused_computation.35 | convolution fusion | flops 8409084 | bytes 2154512 | tf_op jit(solution)/shard_map/dot_general | solution.py:345
  52.0 0.2 multiply_reduce_fusion
  52.2 0.0 copy-done.4
  52.2 0.6 multiply_convert_fusion
  52.9 9.3 %all_to_all.21 = bf16[8,4,1024]{2,1,0:T(4,128)(2,1)S(1)} all-to-all(bf16[8,4,1024]{2,1,0:T(4,128)(2,1)S(1)} %broadcast_in_dim.4), channel_id=1, replica_groups={{0,2,4,6,8,10,12,14},{1,3,5,7,9,11,13,15},{16,18,20,22,24,26,28,30},{17..., dimensions={0} | all-to-all | bytes 131072 | tf_op jit(solution)/shard_map/all_to_all | solution.py:301
  62.2 0.2 fusion.19
  62.4 0.2 broadcast_select_fusion.3
  62.6 10.6 %all_to_all.22 = bf16[8,32,512]{2,1,0:T(8,128)(2,1)S(1)} all-to-all(bf16[8,32,512]{2,1,0:T(8,128)(2,1)S(1)} %broadcast_in_dim.5), channel_id=1, replica_groups={{0,2,4,6,8,10,12,14},{1,3,5,7,9,11,13,15},{16,18,20,22,24,26,28,30},{17..., dimensions={0} | all-to-all | bytes 524288 | tf_op jit(solution)/shard_map/all_to_all | solution.py:301
  73.3 0.1 collective-permute-start.1
  73.4 0.5 convolution_convert_fusion.1
  73.9 1.0 %collective-permute-done.1 = bf16[8,32,512]{2,1,0:T(8,128)(2,1)S(1)} collective-permute-done((bf16[8,32,512]{2,1,0:T(8,128)(2,1)S(1)}, bf16[8,32,512]{2,1,0:T(8,128)(2,1)S(1)}, u32[]{:S(2)}, u32[]{:S(2)}) %collective-permute-start.1) | collective-permute-done | bytes 262176 | tf_op jit(solution)/shard_map/ppermute | solution.py:305
  74.9 0.5 broadcast_select_fusion.1
  75.5 0.6 reshape.101
  (16 shorter events, 0.3 us)
Async XLA Ops:
  0.6 72.8 %copy-start = (bf16[4096,256]{1,0:T(8,128)(2,1)S(1)}, bf16[4096,256]{1,0:T(8,128)(2,1)}, u32[]{:S(2)}) copy-start(bf16[4096,256]{1,0:T(8,128)(2,1)} %param.21) | copy-start | bytes 6291460
  0.6 20.8 %collective-permute-start = (bf16[1024,256]{1,0:T(8,128)(2,1)}, bf16[1024,256]{1,0:T(8,128)(2,1)S(1)}, u32[]{:S(2)}, u32[]{:S(2)}) collective-permute-start(bf16[1024,256]{1,0:T(8,128)(2,1)} %param.20), channel_id=1, source_target_pairs={{0,1},{1,0},{2,3},{3,2},{4,5},{5,4},{6,7},{7,6},{8,9},{9,8},{10,11... | collective-permute-start | bytes 1572872 | tf_op jit(solution)/shard_map/ppermute | solution.py:305
  6.4 15.0 %all-to-all-start = ((bf16[16,4,1024]{2,1,0:T(4,128)(2,1)}), bf16[16,4,1024]{2,1,0:T(4,128)(2,1)S(1)}, u32[]{:S(2)}, u32[]{:S(2)}) async-start(bf16[16,4,1024]{2,1,0:T(4,128)(2,1)} %copies.1), calls=%async_computation | async-start | bytes 262144 | tf_op jit(solution)/shard_map/all_to_all | solution.py:292
  13.5 8.0 %copy-start.1 = (f32[1024]{0:T(1024)S(1)}, f32[1024]{0:T(1024)}, u32[]{:S(2)}) copy-start(f32[1024]{0:T(1024)} %param.13) | copy-start | bytes 12292
  21.4 28.5 %copy-start.3 = (bf16[4,1024]{1,0:T(4,128)(2,1)S(1)}, bf16[4,1024]{1,0:T(4,128)(2,1)}, u32[]{:S(2)}) copy-start(bf16[4,1024]{1,0:T(4,128)(2,1)} %x_hbm.3) | copy-start | bytes 24580
  35.9 16.3 %copy-start.4 = (f32[1024]{0:T(1024)S(1)}, f32[1024]{0:T(1024)}, u32[]{:S(2)}) copy-start(f32[1024]{0:T(1024)} %param.15) | copy-start | bytes 12292
  36.0 26.2 %copy-start.2 = (bf16[1024,256]{1,0:T(8,128)(2,1)S(1)}, bf16[1024,256]{1,0:T(8,128)(2,1)}, u32[]{:S(2)}) copy-start(bf16[1024,256]{1,0:T(8,128)(2,1)} %param.20) | copy-start | bytes 1572868
  73.3 1.6 %collective-permute-start.1 = (bf16[8,32,512]{2,1,0:T(8,128)(2,1)S(1)}, bf16[8,32,512]{2,1,0:T(8,128)(2,1)S(1)}, u32[]{:S(2)}, u32[]{:S(2)}) collective-permute-start(bf16[8,32,512]{2,1,0:T(8,128)(2,1)S(1)} %all_to_all.22), channel_id=1, source_target_pairs={{0,1},{1,0},{2,3},{3,2},{4,5},{5,4},{6,7},{7,6},{8,9},{9,8},{10,11... | collective-permute-start | bytes 786440 | tf_op jit(solution)/shard_map/ppermute | solution.py:305

commit v7 on v5

--- a/solution.py
+++ b/solution.py
@@ -257,11 +257,12 @@
     return lax.all_to_all(blocks, "page", 0, 0, axis_index_groups=sides, tiled=True)
 
 
-def join_sides(mine, count):
-    theirs = lax.ppermute(mine, "page", [(i, i ^ 1) for i in range(count)])
-    even = lax.axis_index("page") % 2 == 0
-    both = jnp.stack([jnp.where(even, mine, theirs), jnp.where(even, theirs, mine)], axis=1)
-    return both.reshape((count,) + mine.shape[1:])
+def swap_cores(array, count):
+    return lax.ppermute(array, "page", [(i, i ^ 1) for i in range(count)])
+
+
+def by_side(even, mine, theirs, axis):
+    return jnp.concatenate([jnp.where(even, mine, theirs), jnp.where(even, theirs, mine)], axis=axis)
 
 
 def body(
@@ -282,6 +283,10 @@
     lat_all = exchange(spread(latents, count)).reshape(count * lat_rows, width)
     block = math.gcd(patches.shape[0], BLOCK)
     keys, values = early(patches, patch_gain, w_key, w_value, block)
+    even = lax.axis_index("page") % 2 == 0
+    lat_all, w_theirs, even = lax.optimization_barrier(
+        (lat_all, swap_cores(w_hidden, count), even)
+    )
     packed = attend(
         lat_all, lat_gain, w_query, patches, patch_gain, w_key, w_value, keys, values
     )
@@ -298,16 +303,28 @@
     )
     resampled = mixed.astype(jnp.bfloat16)
     mlp_in = norm_rows(mixed, mlp_gain).astype(jnp.bfloat16)
-    mlp_all = exchange(spread(mlp_in, count)).reshape(count * lat_rows, width)
-    hidden = jax.nn.gelu(
-        jnp.dot(mlp_all, w_hidden, preferred_element_type=jnp.float32), approximate=True
-    ).astype(jnp.bfloat16)
-    rows, units = hidden.shape
-    hidden_all = join_sides(exchange_side(spread(hidden, count // 2), count), count)
-    hidden_all = jnp.transpose(hidden_all, (1, 0, 2)).reshape(rows, count * units)
-    connector = jnp.dot(hidden_all, w_connect, preferred_element_type=jnp.float32).astype(
-        jnp.bfloat16
-    )
+    chips = count // 2
+    rows = chips * lat_rows
+    mlp_side = exchange_side(spread(mlp_in, chips), count).reshape(rows, width)
+
+    def hidden_of(weight):
+        return jax.nn.gelu(
+            jnp.dot(mlp_side, weight, preferred_element_type=jnp.float32), approximate=True
+        ).astype(jnp.bfloat16)
+
+    hidden = by_side(even, hidden_of(w_hidden), hidden_of(w_theirs), 1)
+    hidden_mine = exchange_side(spread(hidden, chips), count)
+    hidden_theirs = swap_cores(hidden_mine, count)
+
+    def connect(blocks):
+        flat = jnp.transpose(blocks, (1, 0, 2)).reshape(rows, w_connect.shape[0])
+        return jnp.dot(flat, w_connect, preferred_element_type=jnp.float32).astype(jnp.bfloat16)
+
+    sides = [
+        part.reshape(chips, 1, lat_rows, w_connect.shape[1])
+        for part in (connect(hidden_mine), connect(hidden_theirs))
+    ]
+    connector = by_side(even, sides[0], sides[1], 1).reshape(count * lat_rows, w_connect.shape[1])
     return (resampled, connector)
 
 

time: 70.4 us -> 68.9 us (0.979)
  blocking collectives: 33.5 us -> 31.7 us
    all_to_all x2 -> x1, blocking collectives: 22.3 us -> 11.8 us  [exchange(): return lax.all_to_all(blocks, 'page', 0, 0, tiled=True)]
    all_to_all x1 -> x2, blocking collectives: 11.2 us -> 19.9 us  [exchange_side(): lax.all_to_all(blocks, 'page', 0, 0, axis_index_groups=sides, tiled=True)]
    ppermute x1 -> x2, waiting for transfers between devices: 1.53 us -> 1.05 us  [swap_cores(): return lax.ppermute(array, 'page', [(i, i ^ 1) for i in range(count)])]
  transfers between devices with their start and end apart: 2 -> 3, of which waited for: 2 -> 2; matrix products, arithmetic and copies ran while one was open for 0% -> 3% of each run, Pallas kernels for 8% -> 8%
where the time goes in v7:
time: 68.9 us; the launch traced here: 68.5 us
  blocking collectives  31.7 us (46%)
  Pallas kernels  18 us (26%)
  starting transfers between devices  7.58 us (11%)
  waiting for transfers between devices  3.44 us (5%)
  matrix products  3.43 us (5%)
  local copies, waits for them, and re-layouts  2.52 us (4%)
  other arithmetic  1 us (1%)
  between operations  0.84 us (1%)
    all_to_all x2, blocking collectives, exchange_side(): lax.all_to_all(blocks, 'page', 0, 0, axis_index_groups=sides, tiled=True)  19.9 us
    pallas_call x1, Pallas kernels, attend(): pl.pallas_call(attend_kernel, in_specs=[vmem, vmem] + [hbm] * 7, out_spec...  12.5 us
    all_to_all x1, blocking collectives, exchange(): return lax.all_to_all(blocks, 'page', 0, 0, tiled=True)  11.8 us
    all_to_all x1, starting transfers between devices, exchange(): return lax.all_to_all(blocks, 'page', 0, 0, tiled=True)  6.99 us
    pallas_call x1, Pallas kernels, early(): pl.pallas_call(early_kernel, in_specs=[hbm] * 4, out_specs=[hbm] * 2, out...  5.52 us
    all_to_all x1, waiting for transfers between devices, exchange(): return lax.all_to_all(blocks, 'page', 0, 0, tiled=True)  2.39 us
    dot_general x1, matrix products, body(): jnp.dot(attended, w_out, preferred_element_type=jnp.float32)  2.09 us
    broadcast_in_dim x3, local copies, waits for them, and re-layouts, spread(): return jnp.broadcast_to(block[None], (count,) + block.shape)  1.53 us
  transfers between devices with their start and end apart: 3, of which 2 were waited for; matrix products, arithmetic and copies ran while one was open for 3% of the time, Pallas kernels for 8%

profile of v7, /device:TPU:0, one launch (start us, length us, event | category | flops | bytes accessed | tf_op | source)
XLA Modules:
  0.0 68.5 jit_solution(18135280193672154602)
XLA Ops:
  0.6 0.0 copy-start
  0.6 0.5 collective-permute-start
  1.2 1.5 %broadcast_in_dim.6 = bf16[16,4,1024]{2,1,0:T(4,128)(2,1)} broadcast(bf16[4,1024]{1,0:T(4,128)(2,1)} %param.11), dimensions={1,2} | broadcast | bytes 139264 | tf_op jit(solution)/shard_map/broadcast_in_dim | solution.py:252
  2.6 7.0 %all-to-all-start = ((bf16[16,4,1024]{2,1,0:T(4,128)(2,1)}), bf16[16,4,1024]{2,1,0:T(4,128)(2,1)S(1)}, u32[]{:S(2)}, u32[]{:S(2)}) async-start(bf16[16,4,1024]{2,1,0:T(4,128)(2,1)} %broadcast_in_dim.6), calls=%async_computation | async-start | bytes 262144 | tf_op jit(solution)/shard_map/all_to_all | solution.py:248
  9.7 0.0 copy-start.1
  9.7 5.5 %early.1 = (bf16[512,1024]{1,0:T(8,128)(2,1)}, bf16[512,1024]{1,0:T(8,128)(2,1)}) custom-call(bf16[2048,1024]{1,0:T(8,128)(2,1)} %x_hbm.3, f32[1,1024]{1,0:T(1,128)} %bitcast.22, bf16[1024,1024]{1,0:T(8,128)(2,1)} %wk_hbm.3, bf16[1024,1024]{1,0:T(8,128)(2,1)} %wv_hbm.3), custom_call_target="tpu_custom_call" | custom-call | flops 2147483648 | bytes 7340032 | tf_op jit(solution)/shard_map/early/pallas_call | solution.py:82
  15.2 2.4 %all-to-all-done = bf16[16,4,1024]{2,1,0:T(4,128)(2,1)S(1)} async-done(((bf16[16,4,1024]{2,1,0:T(4,128)(2,1)}), bf16[16,4,1024]{2,1,0:T(4,128)(2,1)S(1)}, u32[]{:S(2)}, u32[]{:S(2)}) %all-to-all-start) | async-done | bytes 131104 | tf_op jit(solution)/shard_map/all_to_all | solution.py:248
  17.6 0.0 collective-permute-done
  17.6 0.0 copy-done.1
  17.6 0.0 copy-start.3
  17.7 12.5 %attend.1 = bf16[64,1152]{1,0:T(8,128)(2,1)S(1)} custom-call(bf16[64,1024]{1,0:T(8,128)(2,1)S(1)} %reshape.95.lat_ref, f32[1,1024]{1,0:T(1,128)S(1)} %bitcast.17, bf16[1024,1024]{1,0:T(8,128)(2,1)} %wq_hbm.1, bf16[2048,1024]{1,0:T(8,128)(2,1)} %x_hbm.3, f32[1,1024]{1,0:T(1,128)} %bitcast.23, bf16[1024,1024]{1,0:T(8,128)(2,1)} %wk_hbm.3, ...), custom_call_target="tpu_custom_call" | custom-call | flops 8589934592 | bytes 10485760 | tf_op jit(solution)/shard_map/attend/pallas_call | solution.py:210
  30.2 0.0 copy-start.4
  30.2 0.0 copy-start.2
  30.2 11.8 %all_to_all.20 = bf16[16,4,1152]{2,1,0:T(4,128)(2,1)S(1)} all-to-all(bf16[16,4,1152]{2,1,0:T(4,128)(2,1)S(1)} %reshape.98), channel_id=1, replica_groups=mesh['slab'=2,'page'=16] {'page'}, dimensions={0} | all-to-all | bytes 294912 | tf_op jit(solution)/shard_map/all_to_all | solution.py:248
  42.0 0.1 convert_reduce_fusion
  42.1 0.1 slice_add_fusion
  42.1 0.1 div.17
  42.2 0.1 div.18
  42.3 0.0 copy-done.3
  42.3 2.1 %fusion.18 = (f32[4]{0:T(128)S(1)}, f32[4,1024]{1,0:T(4,128)S(1)}) fusion(bf16[1024,1024]{1,0:T(8,128)(2,1)} %param.19, f32[4,1024]{1,0:T(4,128)S(1)} %div.18, f32[4,1152]{1,0:T(4,128)S(1)} %convert_reduce_fusion, bf16[4,1024]{1,0:T(4,128)(2,1)S(1)} %copy-done.3), kind=kOutput, calls=%fused_computation.35 | convolution fusion | flops 8409084 | bytes 2154512 | tf_op jit(solution)/shard_map/dot_general | solution.py:301
  44.4 0.2 multiply_reduce_fusion
  44.6 0.0 copy-done.4
  44.6 0.6 multiply_convert_fusion
  45.3 9.3 %all_to_all.21 = bf16[8,4,1024]{2,1,0:T(4,128)(2,1)S(1)} all-to-all(bf16[8,4,1024]{2,1,0:T(4,128)(2,1)S(1)} %broadcast_in_dim.7), channel_id=1, replica_groups={{0,2,4,6,8,10,12,14},{1,3,5,7,9,11,13,15},{16,18,20,22,24,26,28,30},{17..., dimensions={0} | all-to-all | bytes 131072 | tf_op jit(solution)/shard_map/all_to_all | solution.py:257
  54.6 0.2 fusion.19
  54.8 0.2 broadcast_select_fusion.3
  55.0 10.6 %all_to_all.22 = bf16[8,32,512]{2,1,0:T(8,128)(2,1)S(1)} all-to-all(bf16[8,32,512]{2,1,0:T(8,128)(2,1)S(1)} %broadcast_in_dim.8), channel_id=1, replica_groups={{0,2,4,6,8,10,12,14},{1,3,5,7,9,11,13,15},{16,18,20,22,24,26,28,30},{17..., dimensions={0} | all-to-all | bytes 524288 | tf_op jit(solution)/shard_map/all_to_all | solution.py:257
  65.7 0.1 collective-permute-start.1
  65.8 0.5 convolution_convert_fusion.1
  66.2 1.0 %collective-permute-done.1 = bf16[8,32,512]{2,1,0:T(8,128)(2,1)S(1)} collective-permute-done((bf16[8,32,512]{2,1,0:T(8,128)(2,1)S(1)}, bf16[8,32,512]{2,1,0:T(8,128)(2,1)S(1)}, u32[]{:S(2)}, u32[]{:S(2)}) %collective-permute-start.1) | collective-permute-done | bytes 262176 | tf_op jit(solution)/shard_map/ppermute | solution.py:261
  67.3 0.5 broadcast_select_fusion.1
  67.9 0.6 reshape.102
  (16 shorter events, 0.3 us)
Async XLA Ops:
  0.6 65.1 %copy-start = (bf16[4096,256]{1,0:T(8,128)(2,1)S(1)}, bf16[4096,256]{1,0:T(8,128)(2,1)}, u32[]{:S(2)}) copy-start(bf16[4096,256]{1,0:T(8,128)(2,1)} %param.21) | copy-start | bytes 6291460
  0.6 17.0 %collective-permute-start = (bf16[1024,256]{1,0:T(8,128)(2,1)}, bf16[1024,256]{1,0:T(8,128)(2,1)S(1)}, u32[]{:S(2)}, u32[]{:S(2)}) collective-permute-start(bf16[1024,256]{1,0:T(8,128)(2,1)} %param.20), channel_id=1, source_target_pairs={{0,1},{1,0},{2,3},{3,2},{4,5},{5,4},{6,7},{7,6},{8,9},{9,8},{10,11... | collective-permute-start | bytes 1572872 | tf_op jit(solution)/shard_map/ppermute | solution.py:261
  2.6 14.9 %all-to-all-start = ((bf16[16,4,1024]{2,1,0:T(4,128)(2,1)}), bf16[16,4,1024]{2,1,0:T(4,128)(2,1)S(1)}, u32[]{:S(2)}, u32[]{:S(2)}) async-start(bf16[16,4,1024]{2,1,0:T(4,128)(2,1)} %broadcast_in_dim.6), calls=%async_computation | async-start | bytes 262144 | tf_op jit(solution)/shard_map/all_to_all | solution.py:248
  9.7 8.0 %copy-start.1 = (f32[1024]{0:T(1024)S(1)}, f32[1024]{0:T(1024)}, u32[]{:S(2)}) copy-start(f32[1024]{0:T(1024)} %param.13) | copy-start | bytes 12292
  17.6 24.7 %copy-start.3 = (bf16[4,1024]{1,0:T(4,128)(2,1)S(1)}, bf16[4,1024]{1,0:T(4,128)(2,1)}, u32[]{:S(2)}) copy-start(bf16[4,1024]{1,0:T(4,128)(2,1)} %param.11) | copy-start | bytes 24580
  30.2 14.4 %copy-start.4 = (f32[1024]{0:T(1024)S(1)}, f32[1024]{0:T(1024)}, u32[]{:S(2)}) copy-start(f32[1024]{0:T(1024)} %param.15) | copy-start | bytes 12292
  30.2 24.4 %copy-start.2 = (bf16[1024,256]{1,0:T(8,128)(2,1)S(1)}, bf16[1024,256]{1,0:T(8,128)(2,1)}, u32[]{:S(2)}) copy-start(bf16[1024,256]{1,0:T(8,128)(2,1)} %param.20) | copy-start | bytes 1572868
  65.7 1.6 %collective-permute-start.1 = (bf16[8,32,512]{2,1,0:T(8,128)(2,1)S(1)}, bf16[8,32,512]{2,1,0:T(8,128)(2,1)S(1)}, u32[]{:S(2)}, u32[]{:S(2)}) collective-permute-start(bf16[8,32,512]{2,1,0:T(8,128)(2,1)S(1)} %all_to_all.22), channel_id=1, source_target_pairs={{0,1},{1,0},{2,3},{3,2},{4,5},{5,4},{6,7},{7,6},{8,9},{9,8},{10,11... | collective-permute-start | bytes 786440 | tf_op jit(solution)/shard_map/ppermute | solution.py:261

commit v8 on v7

--- a/solution.py
+++ b/solution.py
@@ -290,7 +290,12 @@
     packed = attend(
         lat_all, lat_gain, w_query, patches, patch_gain, w_key, w_value, keys, values
     )
-    parts = exchange(packed.reshape(count, lat_rows, width + LANES))
+    chips = count // 2
+    packed = packed.reshape(chips, 2, lat_rows, width + LANES)
+    keep = jnp.where(even, packed[:, 0], packed[:, 1])
+    give = jnp.where(even, packed[:, 1], packed[:, 0])
+    pair = keep.astype(jnp.float32) + swap_cores(give, count).astype(jnp.float32)
+    parts = exchange_side(pair.astype(jnp.bfloat16), count)
     summed = jnp.sum(parts.astype(jnp.float32), axis=0)
     denom = summed[:, width : width + HEADS] + summed[:, width + HEADS : width + 2 * HEADS]
     attended = (
@@ -303,7 +308,6 @@
     )
     resampled = mixed.astype(jnp.bfloat16)
     mlp_in = norm_rows(mixed, mlp_gain).astype(jnp.bfloat16)
-    chips = count // 2
     rows = chips * lat_rows
     mlp_side = exchange_side(spread(mlp_in, chips), count).reshape(rows, width)
 

time: 68.9 us -> 68.8 us (level)
  blocking collectives: 31.7 us -> 30.2 us
  waiting for transfers between devices: 3.44 us -> 4.67 us
    all_to_all x1 -> x0, blocking collectives: 11.8 us -> none  [exchange(): return lax.all_to_all(blocks, 'page', 0, 0, tiled=True)]
    all_to_all x2 -> x3, blocking collectives: 19.9 us -> 30.2 us  [exchange_side(): lax.all_to_all(blocks, 'page', 0, 0, axis_index_groups=sides, tiled=True)]
    ppermute x2 -> x3, waiting for transfers between devices: 1.05 us -> 2.3 us  [swap_cores(): return lax.ppermute(array, 'page', [(i, i ^ 1) for i in range(count)])]
  transfers between devices with their start and end apart: 3 -> 4, of which waited for: 2 -> 3; matrix products, arithmetic and copies ran while one was open for 3% -> 3% of each run, Pallas kernels for 8% -> 8%
where the time goes in v8:
time: 68.8 us; the launch traced here: 68.4 us
  blocking collectives  30.2 us (44%)
  Pallas kernels  18 us (26%)
  starting transfers between devices  7.65 us (11%)
  waiting for transfers between devices  4.67 us (7%)
  matrix products  3.43 us (5%)
  local copies, waits for them, and re-layouts  2.52 us (4%)
  other arithmetic  1.07 us (2%)
  between operations  0.86 us (1%)
    all_to_all x3, blocking collectives, exchange_side(): lax.all_to_all(blocks, 'page', 0, 0, axis_index_groups=sides, tiled=True)  30.2 us
    pallas_call x1, Pallas kernels, attend(): pl.pallas_call(attend_kernel, in_specs=[vmem, vmem] + [hbm] * 7, out_spec...  12.5 us
    all_to_all x1, starting transfers between devices, exchange(): return lax.all_to_all(blocks, 'page', 0, 0, tiled=True)  6.99 us
    pallas_call x1, Pallas kernels, early(): pl.pallas_call(early_kernel, in_specs=[hbm] * 4, out_specs=[hbm] * 2, out...  5.54 us
    all_to_all x1, waiting for transfers between devices, exchange(): return lax.all_to_all(blocks, 'page', 0, 0, tiled=True)  2.37 us
    ppermute x3, waiting for transfers between devices, swap_cores(): return lax.ppermute(array, 'page', [(i, i ^ 1) for i in range(count)])  2.3 us
    dot_general x1, matrix products, body(): jnp.dot(attended, w_out, preferred_element_type=jnp.float32)  2.09 us
    broadcast_in_dim x3, local copies, waits for them, and re-layouts, spread(): return jnp.broadcast_to(block[None], (count,) + block.shape)  1.52 us
  transfers between devices with their start and end apart: 4, of which 3 were waited for; matrix products, arithmetic and copies ran while one was open for 3% of the time, Pallas kernels for 8%

profile of v8, /device:TPU:0, one launch (start us, length us, event | category | flops | bytes accessed | tf_op | source)
XLA Modules:
  0.0 68.4 jit_solution(976791701870931107)
XLA Ops:
  0.6 0.0 copy-start
  0.6 0.5 collective-permute-start
  1.2 1.5 %broadcast_in_dim.6 = bf16[16,4,1024]{2,1,0:T(4,128)(2,1)} broadcast(bf16[4,1024]{1,0:T(4,128)(2,1)} %param.11), dimensions={1,2} | broadcast | bytes 139264 | tf_op jit(solution)/shard_map/broadcast_in_dim | solution.py:252
  2.6 7.0 %all-to-all-start = ((bf16[16,4,1024]{2,1,0:T(4,128)(2,1)}), bf16[16,4,1024]{2,1,0:T(4,128)(2,1)S(1)}, u32[]{:S(2)}, u32[]{:S(2)}) async-start(bf16[16,4,1024]{2,1,0:T(4,128)(2,1)} %broadcast_in_dim.6), calls=%async_computation | async-start | bytes 262144 | tf_op jit(solution)/shard_map/all_to_all | solution.py:248
  9.7 0.0 copy-start.1
  9.7 5.5 %early.1 = (bf16[512,1024]{1,0:T(8,128)(2,1)}, bf16[512,1024]{1,0:T(8,128)(2,1)}) custom-call(bf16[2048,1024]{1,0:T(8,128)(2,1)} %x_hbm.3, f32[1,1024]{1,0:T(1,128)} %bitcast.43, bf16[1024,1024]{1,0:T(8,128)(2,1)} %wk_hbm.3, bf16[1024,1024]{1,0:T(8,128)(2,1)} %wv_hbm.3), custom_call_target="tpu_custom_call" | custom-call | flops 2147483648 | bytes 7340032 | tf_op jit(solution)/shard_map/early/pallas_call | solution.py:82
  15.2 2.4 %all-to-all-done = bf16[16,4,1024]{2,1,0:T(4,128)(2,1)S(1)} async-done(((bf16[16,4,1024]{2,1,0:T(4,128)(2,1)}), bf16[16,4,1024]{2,1,0:T(4,128)(2,1)S(1)}, u32[]{:S(2)}, u32[]{:S(2)}) %all-to-all-start) | async-done | bytes 131104 | tf_op jit(solution)/shard_map/all_to_all | solution.py:248
  17.6 0.0 collective-permute-done
  17.6 0.0 copy-start.3
  17.7 12.5 %attend.1 = bf16[64,1152]{1,0:T(8,128)(2,1)S(1)} custom-call(bf16[64,1024]{1,0:T(8,128)(2,1)S(1)} %reshape.101.lat_ref, f32[1,1024]{1,0:T(1,128)S(1)} %bitcast.38, bf16[1024,1024]{1,0:T(8,128)(2,1)} %wq_hbm.1, bf16[2048,1024]{1,0:T(8,128)(2,1)} %x_hbm.3, f32[1,1024]{1,0:T(1,128)} %bitcast.44, bf16[1024,1024]{1,0:T(8,128)(2,1)} %wk_hbm.3, ...), custom_call_target="tpu_custom_call" | custom-call | flops 8589934592 | bytes 10485760 | tf_op jit(solution)/shard_map/attend/pallas_call | solution.py:210
  30.2 0.0 copy-start.4
  30.2 0.0 copy-start.2
  30.3 0.1 collective-permute-start.1
  30.4 1.3 %collective-permute-done.1 = bf16[8,4,1152]{2,1,0:T(4,128)(2,1)S(1)} collective-permute-done((bf16[8,4,1152]{2,1,0:T(4,128)(2,1)S(1)}, bf16[8,4,1152]{2,1,0:T(4,128)(2,1)S(1)}, u32[]{:S(2)}, u32[]{:S(2)}) %collective-permute-start.1) | collective-permute-done | bytes 73760 | tf_op jit(solution)/shard_map/ppermute | solution.py:261
  31.6 0.1 fusion
  31.7 10.3 %all_to_all.20 = bf16[8,4,1152]{2,1,0:T(4,128)(2,1)S(1)} all-to-all(bf16[8,4,1152]{2,1,0:T(4,128)(2,1)S(1)} %fusion), channel_id=1, replica_groups={{0,2,4,6,8,10,12,14},{1,3,5,7,9,11,13,15},{16,18,20,22,24,26,28,30},{17..., dimensions={0} | all-to-all | bytes 147456 | tf_op jit(solution)/shard_map/all_to_all | solution.py:257
  42.0 0.1 slice_add_fusion
  42.1 0.1 div.17
  42.2 0.1 div.18
  42.2 2.1 %fusion.21 = (f32[4]{0:T(128)S(1)}, f32[4,1024]{1,0:T(4,128)S(1)}) fusion(bf16[1024,1024]{1,0:T(8,128)(2,1)} %param.19, f32[4,1024]{1,0:T(4,128)S(1)} %div.18, f32[4,1152]{1,0:T(4,128)S(1)} %convert_reduce_fusion, bf16[4,1024]{1,0:T(4,128)(2,1)S(1)} %copy-done.3), kind=kOutput, calls=%fused_computation.41 | convolution fusion | flops 8409084 | bytes 2154512 | tf_op jit(solution)/shard_map/dot_general | solution.py:306
  44.3 0.2 multiply_reduce_fusion
  44.5 0.0 copy-done.4
  44.6 0.6 multiply_convert_fusion
  45.2 9.3 %all_to_all.21 = bf16[8,4,1024]{2,1,0:T(4,128)(2,1)S(1)} all-to-all(bf16[8,4,1024]{2,1,0:T(4,128)(2,1)S(1)} %broadcast_in_dim.7), channel_id=1, replica_groups={{0,2,4,6,8,10,12,14},{1,3,5,7,9,11,13,15},{16,18,20,22,24,26,28,30},{17..., dimensions={0} | all-to-all | bytes 131072 | tf_op jit(solution)/shard_map/all_to_all | solution.py:257
  54.5 0.2 fusion.22
  54.7 0.2 broadcast_select_fusion.3
  55.0 10.6 %all_to_all.22 = bf16[8,32,512]{2,1,0:T(8,128)(2,1)S(1)} all-to-all(bf16[8,32,512]{2,1,0:T(8,128)(2,1)S(1)} %broadcast_in_dim.8), channel_id=1, replica_groups={{0,2,4,6,8,10,12,14},{1,3,5,7,9,11,13,15},{16,18,20,22,24,26,28,30},{17..., dimensions={0} | all-to-all | bytes 524288 | tf_op jit(solution)/shard_map/all_to_all | solution.py:257
  65.6 0.1 collective-permute-start.2
  65.7 0.5 convolution_convert_fusion.1
  66.2 1.0 %collective-permute-done.2 = bf16[8,32,512]{2,1,0:T(8,128)(2,1)S(1)} collective-permute-done((bf16[8,32,512]{2,1,0:T(8,128)(2,1)S(1)}, bf16[8,32,512]{2,1,0:T(8,128)(2,1)S(1)}, u32[]{:S(2)}, u32[]{:S(2)}) %collective-permute-start.2) | collective-permute-done | bytes 262176 | tf_op jit(solution)/shard_map/ppermute | solution.py:261
  67.3 0.5 broadcast_select_fusion.1
  67.8 0.6 reshape.108
  (20 shorter events, 0.4 us)
Async XLA Ops:
  0.6 65.1 %copy-start = (bf16[4096,256]{1,0:T(8,128)(2,1)S(1)}, bf16[4096,256]{1,0:T(8,128)(2,1)}, u32[]{:S(2)}) copy-start(bf16[4096,256]{1,0:T(8,128)(2,1)} %param.21) | copy-start | bytes 6291460
  0.6 17.0 %collective-permute-start = (bf16[1024,256]{1,0:T(8,128)(2,1)}, bf16[1024,256]{1,0:T(8,128)(2,1)S(1)}, u32[]{:S(2)}, u32[]{:S(2)}) collective-permute-start(bf16[1024,256]{1,0:T(8,128)(2,1)} %param.20), channel_id=1, source_target_pairs={{0,1},{1,0},{2,3},{3,2},{4,5},{5,4},{6,7},{7,6},{8,9},{9,8},{10,11... | collective-permute-start | bytes 1572872 | tf_op jit(solution)/shard_map/ppermute | solution.py:261
  2.6 14.9 %all-to-all-start = ((bf16[16,4,1024]{2,1,0:T(4,128)(2,1)}), bf16[16,4,1024]{2,1,0:T(4,128)(2,1)S(1)}, u32[]{:S(2)}, u32[]{:S(2)}) async-start(bf16[16,4,1024]{2,1,0:T(4,128)(2,1)} %broadcast_in_dim.6), calls=%async_computation | async-start | bytes 262144 | tf_op jit(solution)/shard_map/all_to_all | solution.py:248
  9.7 8.0 %copy-start.1 = (f32[1024]{0:T(1024)S(1)}, f32[1024]{0:T(1024)}, u32[]{:S(2)}) copy-start(f32[1024]{0:T(1024)} %param.13) | copy-start | bytes 12292
  17.6 24.6 %copy-start.3 = (bf16[4,1024]{1,0:T(4,128)(2,1)S(1)}, bf16[4,1024]{1,0:T(4,128)(2,1)}, u32[]{:S(2)}) copy-start(bf16[4,1024]{1,0:T(4,128)(2,1)} %param.11) | copy-start | bytes 24580
  30.2 14.4 %copy-start.4 = (f32[1024]{0:T(1024)S(1)}, f32[1024]{0:T(1024)}, u32[]{:S(2)}) copy-start(f32[1024]{0:T(1024)} %param.15) | copy-start | bytes 12292
  30.2 24.3 %copy-start.2 = (bf16[1024,256]{1,0:T(8,128)(2,1)S(1)}, bf16[1024,256]{1,0:T(8,128)(2,1)}, u32[]{:S(2)}) copy-start(bf16[1024,256]{1,0:T(8,128)(2,1)} %param.20) | copy-start | bytes 1572868
  30.3 1.3 %collective-permute-start.1 = (bf16[8,4,1152]{2,1,0:T(4,128)(2,1)S(1)}, bf16[8,4,1152]{2,1,0:T(4,128)(2,1)S(1)}, u32[]{:S(2)}, u32[]{:S(2)}) collective-permute-start(bf16[8,4,1152]{2,1,0:T(4,128)(2,1)S(1)} %fusion.1), channel_id=1, source_target_pairs={{0,1},{1,0},{2,3},{3,2},{4,5},{5,4},{6,7},{7,6},{8,9},{9,8},{10,11... | collective-permute-start | bytes 221192 | tf_op jit(solution)/shard_map/ppermute | solution.py:261
  65.6 1.6 %collective-permute-start.2 = (bf16[8,32,512]{2,1,0:T(8,128)(2,1)S(1)}, bf16[8,32,512]{2,1,0:T(8,128)(2,1)S(1)}, u32[]{:S(2)}, u32[]{:S(2)}) collective-permute-start(bf16[8,32,512]{2,1,0:T(8,128)(2,1)S(1)} %all_to_all.22), channel_id=1, source_target_pairs={{0,1},{1,0},{2,3},{3,2},{4,5},{5,4},{6,7},{7,6},{8,9},{9,8},{10,11... | collective-permute-start | bytes 786440 | tf_op jit(solution)/shard_map/ppermute | solution.py:261

commit v9 on v8

--- a/solution.py
+++ b/solution.py
@@ -284,9 +284,7 @@
     block = math.gcd(patches.shape[0], BLOCK)
     keys, values = early(patches, patch_gain, w_key, w_value, block)
     even = lax.axis_index("page") % 2 == 0
-    lat_all, w_theirs, even = lax.optimization_barrier(
-        (lat_all, swap_cores(w_hidden, count), even)
-    )
+    lat_all, even = lax.optimization_barrier((lat_all, even))
     packed = attend(
         lat_all, lat_gain, w_query, patches, patch_gain, w_key, w_value, keys, values
     )
@@ -294,7 +292,9 @@
     packed = packed.reshape(chips, 2, lat_rows, width + LANES)
     keep = jnp.where(even, packed[:, 0], packed[:, 1])
     give = jnp.where(even, packed[:, 1], packed[:, 0])
-    pair = keep.astype(jnp.float32) + swap_cores(give, count).astype(jnp.float32)
+    give, w_give = lax.optimization_barrier((give, w_hidden))
+    got, w_theirs = lax.optimization_barrier((swap_cores(give, count), swap_cores(w_give, count)))
+    pair = keep.astype(jnp.float32) + got.astype(jnp.float32)
     parts = exchange_side(pair.astype(jnp.bfloat16), count)
     summed = jnp.sum(parts.astype(jnp.float32), axis=0)
     denom = summed[:, width : width + HEADS] + summed[:, width + HEADS : width + 2 * HEADS]

time: 68.8 us -> 70.6 us (1.026)
  matrix products: 3.43 us -> 4.48 us
    dot_general x2, matrix products: 0.41 us -> 1.46 us  [hidden_of(): jnp.dot(mlp_side, weight, preferred_element_type=jnp.float32)]
  transfers between devices with their start and end apart: 4 -> 4, of which waited for: 3 -> 3; matrix products, arithmetic and copies ran while one was open for 3% -> 1% of each run, Pallas kernels for 8% -> 8%
where the time goes in v9:
time: 70.6 us; the launch traced here: 70.2 us
  blocking collectives  30.2 us (43%)
  Pallas kernels  18.1 us (26%)
  starting transfers between devices  8.02 us (11%)
  waiting for transfers between devices  4.95 us (7%)
  matrix products  4.48 us (6%)
  local copies, waits for them, and re-layouts  2.57 us (4%)
  other arithmetic  1.07 us (2%)
  between operations  0.85 us (1%)
    all_to_all x3, blocking collectives, exchange_side(): lax.all_to_all(blocks, 'page', 0, 0, axis_index_groups=sides, tiled=True)  30.2 us
    pallas_call x1, Pallas kernels, attend(): pl.pallas_call(attend_kernel, in_specs=[vmem, vmem] + [hbm] * 7, out_spec...  12.6 us
    all_to_all x1, starting transfers between devices, exchange(): return lax.all_to_all(blocks, 'page', 0, 0, tiled=True)  7.39 us
    pallas_call x1, Pallas kernels, early(): pl.pallas_call(early_kernel, in_specs=[hbm] * 4, out_specs=[hbm] * 2, out...  5.53 us
    ppermute x3, waiting for transfers between devices, swap_cores(): return lax.ppermute(array, 'page', [(i, i ^ 1) for i in range(count)])  2.58 us
    all_to_all x1, waiting for transfers between devices, exchange(): return lax.all_to_all(blocks, 'page', 0, 0, tiled=True)  2.37 us
    dot_general x1, matrix products, body(): jnp.dot(attended, w_out, preferred_element_type=jnp.float32)  2.09 us
    broadcast_in_dim x3, local copies, waits for them, and re-layouts, spread(): return jnp.broadcast_to(block[None], (count,) + block.shape)  1.57 us
  transfers between devices with their start and end apart: 4, of which 3 were waited for; matrix products, arithmetic and copies ran while one was open for 1% of the time, Pallas kernels for 8%

profile of v9, /device:TPU:0, one launch (start us, length us, event | category | flops | bytes accessed | tf_op | source)
XLA Modules:
  0.0 70.2 jit_solution(8387147661109292530)
XLA Ops:
  0.6 0.0 copy-start
  0.6 1.5 %broadcast_in_dim.6 = bf16[16,4,1024]{2,1,0:T(4,128)(2,1)} broadcast(bf16[4,1024]{1,0:T(4,128)(2,1)} %param.11), dimensions={1,2} | broadcast | bytes 139264 | tf_op jit(solution)/shard_map/broadcast_in_dim | solution.py:252
  2.2 7.4 %all-to-all-start = ((bf16[16,4,1024]{2,1,0:T(4,128)(2,1)}), bf16[16,4,1024]{2,1,0:T(4,128)(2,1)S(1)}, u32[]{:S(2)}, u32[]{:S(2)}) async-start(bf16[16,4,1024]{2,1,0:T(4,128)(2,1)} %broadcast_in_dim.6), calls=%async_computation | async-start | bytes 262144 | tf_op jit(solution)/shard_map/all_to_all | solution.py:248
  9.6 0.0 copy-start.1
  9.6 5.5 %early.1 = (bf16[512,1024]{1,0:T(8,128)(2,1)}, bf16[512,1024]{1,0:T(8,128)(2,1)}) custom-call(bf16[2048,1024]{1,0:T(8,128)(2,1)} %x_hbm.3, f32[1,1024]{1,0:T(1,128)} %bitcast.43, bf16[1024,1024]{1,0:T(8,128)(2,1)} %wk_hbm.3, bf16[1024,1024]{1,0:T(8,128)(2,1)} %wv_hbm.3), custom_call_target="tpu_custom_call" | custom-call | flops 2147483648 | bytes 7340032 | tf_op jit(solution)/shard_map/early/pallas_call | solution.py:82
  15.1 2.4 %all-to-all-done = bf16[16,4,1024]{2,1,0:T(4,128)(2,1)S(1)} async-done(((bf16[16,4,1024]{2,1,0:T(4,128)(2,1)}), bf16[16,4,1024]{2,1,0:T(4,128)(2,1)S(1)}, u32[]{:S(2)}, u32[]{:S(2)}) %all-to-all-start) | async-done | bytes 131104 | tf_op jit(solution)/shard_map/all_to_all | solution.py:248
  17.6 0.0 copy-start.2
  17.6 0.0 copy-start.3
  17.6 12.6 %attend.1 = bf16[64,1152]{1,0:T(8,128)(2,1)S(1)} custom-call(bf16[64,1024]{1,0:T(8,128)(2,1)S(1)} %reshape.101.lat_ref, f32[1,1024]{1,0:T(1,128)S(1)} %bitcast.38, bf16[1024,1024]{1,0:T(8,128)(2,1)} %wq_hbm.1, bf16[2048,1024]{1,0:T(8,128)(2,1)} %x_hbm.3, f32[1,1024]{1,0:T(1,128)} %bitcast.44, bf16[1024,1024]{1,0:T(8,128)(2,1)} %wk_hbm.3, ...), custom_call_target="tpu_custom_call" | custom-call | flops 8589934592 | bytes 10485760 | tf_op jit(solution)/shard_map/attend/pallas_call | solution.py:210
  30.1 0.0 copy-start.4
  30.3 0.1 collective-permute-start.1
  30.3 0.5 collective-permute-start
  30.8 1.5 %collective-permute-done = bf16[8,4,1152]{2,1,0:T(4,128)(2,1)S(1)} collective-permute-done((bf16[8,4,1152]{2,1,0:T(4,128)(2,1)S(1)}, bf16[8,4,1152]{2,1,0:T(4,128)(2,1)S(1)}, u32[]{:S(2)}, u32[]{:S(2)}) %collective-permute-start) | collective-permute-done | bytes 73760 | tf_op jit(solution)/shard_map/ppermute | solution.py:261
  32.3 0.0 collective-permute-done.1
  32.4 0.1 fusion
  32.4 10.3 %all_to_all.20 = bf16[8,4,1152]{2,1,0:T(4,128)(2,1)S(1)} all-to-all(bf16[8,4,1152]{2,1,0:T(4,128)(2,1)S(1)} %fusion), channel_id=1, replica_groups={{0,2,4,6,8,10,12,14},{1,3,5,7,9,11,13,15},{16,18,20,22,24,26,28,30},{17..., dimensions={0} | all-to-all | bytes 147456 | tf_op jit(solution)/shard_map/all_to_all | solution.py:257
  42.8 0.1 slice_add_fusion
  42.8 0.1 div.17
  42.9 0.1 div.18
  43.0 2.1 %fusion.21 = (f32[4]{0:T(128)S(1)}, f32[4,1024]{1,0:T(4,128)S(1)}) fusion(bf16[1024,1024]{1,0:T(8,128)(2,1)} %param.19, f32[4,1024]{1,0:T(4,128)S(1)} %div.18, f32[4,1152]{1,0:T(4,128)S(1)} %convert_reduce_fusion, bf16[4,1024]{1,0:T(4,128)(2,1)S(1)} %copy-done.3), kind=kOutput, calls=%fused_computation.41 | convolution fusion | flops 8409084 | bytes 2154512 | tf_op jit(solution)/shard_map/dot_general | solution.py:306
  45.1 0.2 multiply_reduce_fusion
  45.3 0.0 copy-done.4
  45.3 0.6 multiply_convert_fusion
  45.9 9.3 %all_to_all.21 = bf16[8,4,1024]{2,1,0:T(4,128)(2,1)S(1)} all-to-all(bf16[8,4,1024]{2,1,0:T(4,128)(2,1)S(1)} %broadcast_in_dim.7), channel_id=1, replica_groups={{0,2,4,6,8,10,12,14},{1,3,5,7,9,11,13,15},{16,18,20,22,24,26,28,30},{17..., dimensions={0} | all-to-all | bytes 131072 | tf_op jit(solution)/shard_map/all_to_all | solution.py:257
  55.3 0.2 fusion.22
  55.5 1.3 %broadcast_select_fusion.3 = (bf16[32,256]{1,0:T(8,128)(2,1)S(1)}, bf16[32,256]{1,0:T(8,128)(2,1)S(1)}) fusion(pred[]{:T(512)S(6)} %eq.5, f32[32,256]{1,0:T(8,128)S(1)} %fusion.22, bf16[32,1024]{1,0:T(8,128)(2,1)S(1)} %reshape.105, bf16[1024,256]{1,0:T(8,128)(2,1)} %collective-permute-done.1), kind=kOutput, calls=%fused_computation.37 | convolution fusion | flops 16941056 | bytes 655361 | tf_op jit(solution)/shard_map/dot_general | solution.py:316
  56.8 10.6 %all_to_all.22 = bf16[8,32,512]{2,1,0:T(8,128)(2,1)S(1)} all-to-all(bf16[8,32,512]{2,1,0:T(8,128)(2,1)S(1)} %broadcast_in_dim.8), channel_id=1, replica_groups={{0,2,4,6,8,10,12,14},{1,3,5,7,9,11,13,15},{16,18,20,22,24,26,28,30},{17..., dimensions={0} | all-to-all | bytes 524288 | tf_op jit(solution)/shard_map/all_to_all | solution.py:257
  67.4 0.1 collective-permute-start.2
  67.5 0.5 convolution_convert_fusion.1
  68.0 1.0 %collective-permute-done.2 = bf16[8,32,512]{2,1,0:T(8,128)(2,1)S(1)} collective-permute-done((bf16[8,32,512]{2,1,0:T(8,128)(2,1)S(1)}, bf16[8,32,512]{2,1,0:T(8,128)(2,1)S(1)}, u32[]{:S(2)}, u32[]{:S(2)}) %collective-permute-start.2) | collective-permute-done | bytes 262176 | tf_op jit(solution)/shard_map/ppermute | solution.py:261
  69.0 0.5 broadcast_select_fusion.1
  69.6 0.6 reshape.108
  (20 shorter events, 0.4 us)
Async XLA Ops:
  0.6 66.9 %copy-start = (bf16[4096,256]{1,0:T(8,128)(2,1)S(1)}, bf16[4096,256]{1,0:T(8,128)(2,1)}, u32[]{:S(2)}) copy-start(bf16[4096,256]{1,0:T(8,128)(2,1)} %param.21) | copy-start | bytes 6291460
  2.2 15.3 %all-to-all-start = ((bf16[16,4,1024]{2,1,0:T(4,128)(2,1)}), bf16[16,4,1024]{2,1,0:T(4,128)(2,1)S(1)}, u32[]{:S(2)}, u32[]{:S(2)}) async-start(bf16[16,4,1024]{2,1,0:T(4,128)(2,1)} %broadcast_in_dim.6), calls=%async_computation | async-start | bytes 262144 | tf_op jit(solution)/shard_map/all_to_all | solution.py:248
  9.6 8.0 %copy-start.1 = (f32[1024]{0:T(1024)S(1)}, f32[1024]{0:T(1024)}, u32[]{:S(2)}) copy-start(f32[1024]{0:T(1024)} %param.13) | copy-start | bytes 12292
  17.6 12.7 %copy-start.2 = (bf16[1024,256]{1,0:T(8,128)(2,1)S(1)}, bf16[1024,256]{1,0:T(8,128)(2,1)}, u32[]{:S(2)}) copy-start(bf16[1024,256]{1,0:T(8,128)(2,1)} %param.20) | copy-start | bytes 1572868
  17.6 25.4 %copy-start.3 = (bf16[4,1024]{1,0:T(4,128)(2,1)S(1)}, bf16[4,1024]{1,0:T(4,128)(2,1)}, u32[]{:S(2)}) copy-start(bf16[4,1024]{1,0:T(4,128)(2,1)} %param.11) | copy-start | bytes 24580
  30.1 15.2 %copy-start.4 = (f32[1024]{0:T(1024)S(1)}, f32[1024]{0:T(1024)}, u32[]{:S(2)}) copy-start(f32[1024]{0:T(1024)} %param.15) | copy-start | bytes 12292
  30.3 2.1 %collective-permute-start.1 = (bf16[1024,256]{1,0:T(8,128)(2,1)S(1)}, bf16[1024,256]{1,0:T(8,128)(2,1)}, u32[]{:S(2)}, u32[]{:S(2)}) collective-permute-start(bf16[1024,256]{1,0:T(8,128)(2,1)S(1)} %copy-done.2), channel_id=1, source_target_pairs={{0,1},{1,0},{2,3},{3,2},{4,5},{5,4},{6,7},{7,6},{8,9},{9,8},{10,11... | collective-permute-start | bytes 1572872 | tf_op jit(solution)/shard_map/ppermute | solution.py:261
  30.3 2.0 %collective-permute-start = (bf16[8,4,1152]{2,1,0:T(4,128)(2,1)S(1)}, bf16[8,4,1152]{2,1,0:T(4,128)(2,1)S(1)}, u32[]{:S(2)}, u32[]{:S(2)}) collective-permute-start(bf16[8,4,1152]{2,1,0:T(4,128)(2,1)S(1)} %fusion.1), channel_id=1, source_target_pairs={{0,1},{1,0},{2,3},{3,2},{4,5},{5,4},{6,7},{7,6},{8,9},{9,8},{10,11... | collective-permute-start | bytes 221192 | tf_op jit(solution)/shard_map/ppermute | solution.py:261
  67.4 1.6 %collective-permute-start.2 = (bf16[8,32,512]{2,1,0:T(8,128)(2,1)S(1)}, bf16[8,32,512]{2,1,0:T(8,128)(2,1)S(1)}, u32[]{:S(2)}, u32[]{:S(2)}) collective-permute-start(bf16[8,32,512]{2,1,0:T(8,128)(2,1)S(1)} %all_to_all.22), channel_id=1, source_target_pairs={{0,1},{1,0},{2,3},{3,2},{4,5},{5,4},{6,7},{7,6},{8,9},{9,8},{10,11... | collective-permute-start | bytes 786440 | tf_op jit(solution)/shard_map/ppermute | solution.py:261
